TPU v7x, 32 devices: a whole 2x2x4 slice. The times are simulated.
32 devices in a mesh: groups: 2 (over y), text: 4 (over z), image: 4 (over x, core).
Axes of the slice: x: 2, y: 2, z: 4, core: 2. Of those that a mesh axis runs over, the one named last changes fastest.
Arguments:
- text_states: bfloat16 [1024, 8192], P(('groups', 'text')), parts along dimension 0, may hold values from -6 to 6
- grid_levels: bfloat16 [16384, 8192], P(('groups', 'text'), 'image'), parts along dimension 0, may hold values from -8 to 7, as said below
- round_logits: float32 [16384, 8192], P(('groups', 'text'), 'image'), parts along dimension 0, may hold values from -2 to 2
- column_steps: float32 [16384], P(('groups', 'image')), parts along dimension 0, may hold values from 0.0015 to 0.004
- image_keys: bfloat16 [12808, 1024], P('groups', 'image'), parts along dimension 0, may hold values from -500 to 500
- image_values: bfloat16 [12808, 1024], P('groups', 'image'), parts along dimension 0, may hold values from -6 to 6
- target_out: bfloat16 [1024, 8192], P(('groups', 'text'), 'image'), parts along dimension 0, may hold values from -6 to 6
- doc_images: int32 [6], P('groups'), parts along dimension 0, may hold values from 1 to 2, as said below
- image_start: int32 [8], P('groups'), parts along dimension 0, may hold values from 1 to 3, as said below
Outputs:
- rounding_grad: float32 [16384, 8192], P(('groups', 'text'), 'image'), parts along dimension 0
There are 2 independent parts, one for each index of `groups`. A program takes and returns all parts, laid end to end along the dimension named above; each array names one. Nothing has to cross between parts.
Inputs may be any that keep to these rules, and one draw needn't show every extreme that they name: `doc_images`: every document holds one image or more, 4 in all; one document holds exactly 2, and no document more. `image_start`: Nondecreasing; the first image's entry is 1 and the last image's 4 - 1. `grid_levels`: whole numbers.
All inputs are finite; a program needn't handle non-finite values.
Results may differ from a plain program's by a relative error of at most 0.015.
Values may be sent and summed in bfloat16 or wider, within the bound.
A program may use at most 256 MiB of HBM per device.

v0:
```python
import jax
import jax.numpy as jnp
from jax import lax
from jax.sharding import PartitionSpec as P

H = 64
KVH = 8
HD = 128
IMAGES = 4
IMG_TOK = 1601
SPAN = 128


def visibility(span_ids, doc_images, image_start, total_spans):
    images = image_start.shape[0]
    documents = doc_images.shape[0]
    doc_ends = jnp.cumsum(doc_images)
    positions = jnp.arange(images, dtype=jnp.int32)
    doc_of = jnp.sum((positions[:, None] >= doc_ends[None, :]).astype(jnp.int32), axis=1)
    doc_index = jnp.arange(documents, dtype=jnp.int32)
    end_of = jnp.sum(jnp.where(doc_index[None, :] == doc_of[:, None], doc_ends[None, :], 0), axis=1)
    stop_at = jnp.sum(
        jnp.where(positions[None, :] == end_of[:, None], image_start[None, :], 0), axis=1
    )
    stop_at = stop_at + jnp.where(end_of >= images, total_spans, 0)
    return (span_ids[:, None] >= image_start[None, :]) & (span_ids[:, None] < stop_at[None, :])


def head_grad(queries, keys, values, target, visible):
    tokens_here = queries.shape[0]
    kv_heads = queries.shape[1]
    per_group = queries.shape[2]
    head_size = queries.shape[3]
    scaling = head_size ** (-0.5)
    shape = (kv_heads, per_group, tokens_here)

    def tile_of(which):
        keys_now = lax.dynamic_slice_in_dim(keys, which * IMG_TOK, IMG_TOK, 0)
        values_now = lax.dynamic_slice_in_dim(values, which * IMG_TOK, IMG_TOK, 0)
        scores = (
            jnp.einsum("tkgd,nkd->kgtn", queries, keys_now, preferred_element_type=jnp.float32)
            * scaling
        )
        return (scores, keys_now, values_now)

    def seen_of(which):
        return lax.dynamic_index_in_dim(visible, which, 1, keepdims=False)

    def forward(which, state):
        seen_rows = seen_of(which)
        running, total, accum = state
        scores, keys_now, values_now = tile_of(which)
        seen = seen_rows[None, None, :]
        peak = jnp.where(seen, jnp.maximum(running, jnp.max(scores, axis=-1)), running)
        weights = jnp.where(seen[..., None], jnp.exp(scores - peak[..., None]), 0.0)
        fade = jnp.exp(running - peak)
        total = total * fade + jnp.sum(weights, axis=-1)
        product = jnp.einsum(
            "kgtn,nkd->kgtd",
            weights.astype(jnp.bfloat16),
            values_now,
            preferred_element_type=jnp.float32,
        )
        return (peak, total, accum * fade[..., None] + product)

    start_state = (
        jnp.full(shape, -1e30, jnp.float32),
        jnp.zeros(shape, jnp.float32),
        jnp.zeros(shape + (head_size,), jnp.float32),
    )
    running, total, accum = lax.fori_loop(0, IMAGES, forward, start_state)
    denom = jnp.maximum(total, 1.0)
    attended = accum / denom[..., None]
    out_grad = (1024.0 * (attended - target)).astype(jnp.bfloat16)
    delta = jnp.sum(out_grad.astype(jnp.float32) * attended, axis=-1)

    def backward(which, grad_acc):
        seen_rows = seen_of(which)
        scores, keys_now, values_now = tile_of(which)
        seen = seen_rows[None, None, :]
        probs = (
            jnp.where(seen[..., None], jnp.exp(scores - running[..., None]), 0.0) / denom[..., None]
        )
        dprob = jnp.einsum(
            "kgtd,nkd->kgtn", out_grad, values_now, preferred_element_type=jnp.float32
        )
        score_grad = (probs * (dprob - delta[..., None]) * scaling).astype(jnp.bfloat16)
        return grad_acc + jnp.einsum(
            "kgtn,nkd->kgtd", score_grad, keys_now, preferred_element_type=jnp.float32
        )

    grad_sum = lax.fori_loop(0, IMAGES, backward, jnp.zeros(shape + (head_size,), jnp.float32))
    return grad_sum.astype(jnp.bfloat16)


def per_device(
    text_states,
    grid_levels,
    round_logits,
    column_steps,
    image_keys,
    image_values,
    target_out,
    doc_images,
    image_start,
):
    tok_dev = text_states.shape[0]
    out_cols = grid_levels.shape[1]
    n_text = lax.axis_size("text")
    per_group = H // KVH
    kvh_dev = image_keys.shape[1] // HD
    sigmoid_v = jax.nn.sigmoid(round_logits)
    soft = 1.2 * sigmoid_v - 0.1
    weight_q = (column_steps[None, :] * (grid_levels.astype(jnp.float32) + soft)).astype(
        jnp.bfloat16
    )
    spread = lax.all_to_all(text_states, "text", split_axis=1, concat_axis=0, tiled=True)
    q_sum = jnp.dot(
        text_states,
        lax.all_gather(weight_q, "text", axis=0, tiled=True),
        preferred_element_type=jnp.float32,
    )
    queries = q_sum.astype(jnp.bfloat16)
    first_token = lax.axis_index("text") * tok_dev
    span_ids = (first_token + jnp.arange(tok_dev, dtype=jnp.int32)) // SPAN
    visible = visibility(span_ids, doc_images, image_start, n_text * tok_dev // SPAN)
    query_tiles = queries.reshape(tok_dev, kvh_dev, per_group, HD)
    key_tiles = image_keys.reshape(image_keys.shape[0], kvh_dev, HD)
    value_tiles = image_values.reshape(image_values.shape[0], kvh_dev, HD)
    target_tiles = (
        target_out.astype(jnp.float32)
        .reshape(tok_dev, kvh_dev, per_group, HD)
        .transpose(1, 2, 0, 3)
    )
    grads = head_grad(query_tiles, key_tiles, value_tiles, target_tiles, visible)
    query_grad = grads.transpose(2, 0, 1, 3).reshape(tok_dev, out_cols)
    weight_grad = lax.dot_general(
        spread,
        lax.all_gather(query_grad, "text", axis=0, tiled=True),
        (((0,), (0,)), ((), ())),
        preferred_element_type=jnp.float32,
    )
    hprime = 1.2 * sigmoid_v * (1.0 - sigmoid_v)
    centered = 2.0 * soft - 1.0
    return (weight_grad * column_steps[None, :] - 4.0 * centered * centered * centered) * hprime


def solution(mesh):
    placed = (
        P(("groups", "text"), None),
        P(("groups", "text"), "image"),
        P(("groups", "text"), "image"),
        P(("groups", "image")),
        P("groups", "image"),
        P("groups", "image"),
        P(("groups", "text"), "image"),
        P("groups"),
        P("groups"),
    )
    return jax.shard_map(
        per_device,
        mesh=mesh,
        in_specs=placed,
        out_specs=P(("groups", "text"), "image"),
        check_vma=False,
    )
```

profile of v0, /device:TPU:0, one launch (start us, length us, event | category | flops | bytes accessed | tf_op | source)
XLA Modules:
  0.0 935.5 jit_solution(14713893510451674385)
XLA Ops:
  6.5 17.6 %copy.62 = f32[2048,2048]{0,1:T(8,128)} copy(f32[2048,2048]{1,0:T(8,128)} %param.15) | data formatting | bytes 33554432 | tf_op args[2]
  24.1 12.3 %copy.61 = bf16[2048,2048]{0,1:T(8,128)(2,1)} copy(bf16[2048,2048]{1,0:T(8,128)(2,1)} %param.14) | data formatting | bytes 16777216 | tf_op args[1]
  36.4 13.9 %multiply_convert_fusion = bf16[2048,2048]{0,1:T(8,128)(2,1)} fusion(bf16[2048,2048]{0,1:T(8,128)(2,1)} %copy.61, f32[2048]{0:T(1024)S(1)} %copy-done.6, f32[2048,2048]{0,1:T(8,128)} %copy.62), kind=kLoop, calls=%fused_computation.48 | loop fusion | flops 37748736 | bytes 33562624 | tf_op jit(solution)/shard_map/convert_element_type | solution.py:114
  50.4 2.5 copy.74
  52.9 6.3 all-to-all-start
  59.4 6.1 copy.63
  65.5 6.1 copy.66
  71.6 5.8 copy.60
  77.4 5.8 copy.69
  84.1 563.4 %all-gather.3.cloned.1.call-done = bf16[8192,2048]{0,1:T(8,128)(2,1)} async-done(((bf16[2048,2048]{0,1:T(8,128)(2,1)}), bf16[8192,2048]{0,1:T(8,128)(2,1)}) %all-gather.3.cloned.1.call-update) | async-done | bytes 33554448 | tf_op jit(solution)/shard_map/all_gather | solution.py:120
  647.5 15.9 %convolution_convert_fusion = bf16[2048,128]{1,0:T(8,128)(2,1)} fusion(bf16[8192,2048]{0,1:T(8,128)(2,1)} %all-gather.3.cloned.1.call-done, bf16[128,8192]{1,0:T(8,128)(2,1)S(1)} %copy-done), kind=kOutput, calls=%fused_computation.50 | convolution fusion | flops 4295229440 | bytes 36175872 | tf_op jit(solution)/shard_map/dot_general | solution.py:118
  663.4 1.3 copy.70
  664.7 94.8 %while.32 = (s32[]{:T(128)}, f32[2,8,128]{2,1,0:T(8,128)S(1)}, f32[2,8,128]{2,1,0:T(8,128)S(1)}, f32[2,8,128,128]{3,2,1,0:T(8,128)}, pred[128,4]{0,1:T(4,128)(4,...) while((s32[]{:T(128)}, f32[2,8,128]{2,1,0:T(8,128)S(1)}, ...), condition=%wide.region_7.8_spmd.clone, body=%wide.region_4.7_spmd.clone.sunk | while | flops 1712357376 | bytes 52192112 | solution.py:71
  664.9 7.8 bitcast_reduce_fusion.2
  672.8 7.3 fusion.70
  680.1 7.5 fusion.72
  687.6 0.9 copy-done.4
  688.6 7.8 bitcast_reduce_fusion.2
  696.4 7.3 fusion.70
  703.7 7.5 fusion.72
  711.3 0.9 copy-done.4
  712.2 7.8 bitcast_reduce_fusion.2
  720.0 7.3 fusion.70
  727.4 7.5 fusion.72
  734.9 0.9 copy-done.4
  735.8 7.8 bitcast_reduce_fusion.2
  743.7 7.3 fusion.70
  751.0 7.5 fusion.72
  758.5 0.9 copy-done.4
  759.5 1.6 copy.67
  761.7 83.7 %while.33 = (s32[]{:T(128)}, f32[2,8,128,128]{3,2,1,0:T(8,128)}, pred[128,4]{0,1:T(4,128)(4,1)S(1)}, bf16[6404,2,128]{2,0,1:T(8,128)(2,1)}, bf16[128,2,8,128]{3,...) while((s32[]{:T(128)}, f32[2,8,128,128]{3,2,1,0:T(8,128)}, ...), condition=%wide.region_10.11_spmd.clone, body=%wide.region_9.10_spmd.clone.sunk | while | flops 2544910336 | bytes 40319100 | solution.py:92
  762.0 7.8 fusion.78
  769.8 12.0 %fusion.79 = f32[2,8,128,128]{3,2,1,0:T(8,128)S(1)} fusion(f32[2,1601,128,8]{2,1,3,0:T(8,128)} %fusion.78, bf16[2,8,128,128]{3,2,1,0:T(8,128)(2,1)S(1)} %get-tuple-element.701, f32[2,8,128]{2,1,0:T(8,128)S(1)} %get-tuple-element.702, f32[2,8,128]{2,1,0:T(8,128)S(1)} %get-tuple-element.699, f32[2,8,128]{2,1,0:T(8,128)S(1)} %get-tuple-element.698, ...), kind=kOutput, calls=%fused_computation.32.clone.1 | convolution fusion | flops 1705525248 | bytes 17467008 | tf_op jit(solution)/shard_map/while/body/eval_jaxpr/kgtn,nkd->kgtd/dot_general | solution.py:88
  781.8 1.0 copy-done.2
  782.8 7.8 fusion.78
  790.7 12.0 %fusion.79 = f32[2,8,128,128]{3,2,1,0:T(8,128)S(1)} fusion(f32[2,1601,128,8]{2,1,3,0:T(8,128)} %fusion.78, bf16[2,8,128,128]{3,2,1,0:T(8,128)(2,1)S(1)} %get-tuple-element.701, f32[2,8,128]{2,1,0:T(8,128)S(1)} %get-tuple-element.702, f32[2,8,128]{2,1,0:T(8,128)S(1)} %get-tuple-element.699, f32[2,8,128]{2,1,0:T(8,128)S(1)} %get-tuple-element.698, ...), kind=kOutput, calls=%fused_computation.32.clone.1 | convolution fusion | flops 1705525248 | bytes 17467008 | tf_op jit(solution)/shard_map/while/body/eval_jaxpr/kgtn,nkd->kgtd/dot_general | solution.py:88
  802.7 1.0 copy-done.2
  803.7 7.8 fusion.78
  811.5 12.0 %fusion.79 = f32[2,8,128,128]{3,2,1,0:T(8,128)S(1)} fusion(f32[2,1601,128,8]{2,1,3,0:T(8,128)} %fusion.78, bf16[2,8,128,128]{3,2,1,0:T(8,128)(2,1)S(1)} %get-tuple-element.701, f32[2,8,128]{2,1,0:T(8,128)S(1)} %get-tuple-element.702, f32[2,8,128]{2,1,0:T(8,128)S(1)} %get-tuple-element.699, f32[2,8,128]{2,1,0:T(8,128)S(1)} %get-tuple-element.698, ...), kind=kOutput, calls=%fused_computation.32.clone.1 | convolution fusion | flops 1705525248 | bytes 17467008 | tf_op jit(solution)/shard_map/while/body/eval_jaxpr/kgtn,nkd->kgtd/dot_general | solution.py:88
  823.6 1.0 copy-done.2
  824.6 7.8 fusion.78
  832.4 12.0 %fusion.79 = f32[2,8,128,128]{3,2,1,0:T(8,128)S(1)} fusion(f32[2,1601,128,8]{2,1,3,0:T(8,128)} %fusion.78, bf16[2,8,128,128]{3,2,1,0:T(8,128)(2,1)S(1)} %get-tuple-element.701, f32[2,8,128]{2,1,0:T(8,128)S(1)} %get-tuple-element.702, f32[2,8,128]{2,1,0:T(8,128)S(1)} %get-tuple-element.699, f32[2,8,128]{2,1,0:T(8,128)S(1)} %get-tuple-element.698, ...), kind=kOutput, calls=%fused_computation.32.clone.1 | convolution fusion | flops 1705525248 | bytes 17467008 | tf_op jit(solution)/shard_map/while/body/eval_jaxpr/kgtn,nkd->kgtd/dot_general | solution.py:88
  844.4 1.0 copy-done.2
  845.4 2.2 copy.73
  847.7 2.9 copy.75
  850.6 42.5 %all-gather.5.cloned.1.call-done = bf16[512,2048]{0,1:T(8,128)(2,1)} async-done(((bf16[128,2048]{0,1:T(8,128)(2,1)}), bf16[512,2048]{0,1:T(8,128)(2,1)}) %all-gather.5.cloned.1.call-update) | async-done | bytes 2097168 | tf_op jit(solution)/shard_map/all_gather | solution.py:139
  893.2 17.9 %fusion.42 = f32[2048,2048]{0,1:T(8,128)} fusion(bf16[512,2048]{0,1:T(8,128)(2,1)} %all-gather.5.cloned.1.call-done, bf16[512,2048]{1,0:T(8,128)(2,1)S(1)} %bitcast.136, f32[2048]{0:T(1024)S(1)} %copy-done.7, f32[2048,2048]{0,1:T(8,128)} %copy.62), kind=kOutput, calls=%fused_computation.47 | convolution fusion | flops 4357881856 | bytes 37756928 | tf_op jit(solution)/shard_map/dot_general | solution.py:137
  911.1 17.6 %copy.76 = f32[2048,2048]{1,0:T(8,128)} copy(f32[2048,2048]{0,1:T(8,128)} %fusion.42) | data formatting | bytes 33554432 | tf_op jit(solution)/shard_map/mul | solution.py:145
  (76 shorter events, 1.9 us)
Async XLA Ops:
  6.5 640.9 %all-gather.3.cloned.1.call-start = ((), (), s32[]{:S(2)}) async-start(), calls=%async_computation.1 | async-start | bytes 41943040 | tf_op jit(solution)/shard_map/all_gather | solution.py:120
  24.1 12.3 %copy-start.6 = (f32[2048]{0:T(1024)S(1)}, f32[2048]{0:T(1024)}, u32[]{:S(2)}) copy-start(f32[2048]{0:T(1024)} %param.16) | copy-start | bytes 24580
  36.4 14.0 %copy-start = (bf16[128,8192]{1,0:T(8,128)(2,1)S(1)}, bf16[128,8192]{1,0:T(8,128)(2,1)}, u32[]{:S(2)}) copy-start(bf16[128,8192]{1,0:T(8,128)(2,1)} %param.13) | copy-start | bytes 6291460
  50.4 8.9 copy-start.9
  52.9 794.8 %all-to-all-start = ((bf16[128,4,2048]{0,2,1:T(8,128)(2,1)}), bf16[128,4,2048]{0,2,1:T(8,128)(2,1)}, u32[]{:S(2)}, u32[]{:S(2)}) async-start(bf16[128,4,2048]{0,2,1:T(8,128)(2,1)} %bitcast.11), calls=%async_computation | async-start | bytes 4194304 | tf_op jit(solution)/shard_map/all_to_all | solution.py:117
  59.2 834.0 %all-gather.5.cloned.1.call-start = ((), (), s32[]{:S(2)}) async-start(), calls=%async_computation.2 | async-start | bytes 2621440 | tf_op jit(solution)/shard_map/all_gather | solution.py:139
  59.4 23.8 %copy-start.5 = (bf16[128,2048]{1,0:T(8,128)(2,1)S(1)}, bf16[128,2048]{1,0:T(8,128)(2,1)}, u32[]{:S(2)}) copy-start(bf16[128,2048]{1,0:T(8,128)(2,1)} %param.19) | copy-start | bytes 1572868
  59.4 24.4 %copy-start.8 = (s32[4]{0:T(128)S(1)}, s32[4]{0:T(128)}, u32[]{:S(2)}) copy-start(s32[4]{0:T(128)} %param.21) | copy-start | bytes 52
  664.9 15.2 %copy-start.3 = (f32[2,8,128,128]{3,2,1,0:T(8,128)S(1)}, f32[2,8,128,128]{3,2,1,0:T(8,128)}, u32[]{:S(2)}) copy-start(f32[2,8,128,128]{3,2,1,0:T(8,128)} %get-tuple-element.644) | copy-start | bytes 3145732 | tf_op jit(solution)/shard_map/while
  687.6 1.0 copy-start.4
  688.6 15.2 %copy-start.3 = (f32[2,8,128,128]{3,2,1,0:T(8,128)S(1)}, f32[2,8,128,128]{3,2,1,0:T(8,128)}, u32[]{:S(2)}) copy-start(f32[2,8,128,128]{3,2,1,0:T(8,128)} %get-tuple-element.644) | copy-start | bytes 3145732 | tf_op jit(solution)/shard_map/while
  711.2 1.0 copy-start.4
  712.2 15.2 %copy-start.3 = (f32[2,8,128,128]{3,2,1,0:T(8,128)S(1)}, f32[2,8,128,128]{3,2,1,0:T(8,128)}, u32[]{:S(2)}) copy-start(f32[2,8,128,128]{3,2,1,0:T(8,128)} %get-tuple-element.644) | copy-start | bytes 3145732 | tf_op jit(solution)/shard_map/while
  734.9 1.0 copy-start.4
  735.8 15.2 %copy-start.3 = (f32[2,8,128,128]{3,2,1,0:T(8,128)S(1)}, f32[2,8,128,128]{3,2,1,0:T(8,128)}, u32[]{:S(2)}) copy-start(f32[2,8,128,128]{3,2,1,0:T(8,128)} %get-tuple-element.644) | copy-start | bytes 3145732 | tf_op jit(solution)/shard_map/while
  758.5 1.0 copy-start.4
  761.7 131.5 %copy-start.7 = (f32[2048]{0:T(1024)S(1)}, f32[2048]{0:T(1024)}, u32[]{:S(2)}) copy-start(f32[2048]{0:T(1024)} %param.16) | copy-start | bytes 24580
  761.9 7.9 copy-start.1
  781.8 1.0 copy-start.2
  782.8 7.8 copy-start.1
  802.7 1.0 copy-start.2
  803.7 7.8 copy-start.1
  823.6 1.0 copy-start.2
  824.6 7.8 copy-start.1
  844.4 1.0 copy-start.2
Sparse Core Ops, SparseCore 0:
  50.5 596.9 all-gather.2
  847.8 45.3 all-gather.4
where the time goes:
time: 937 us; the launch traced here: 935 us
  waiting for transfers between devices  606 us (65%)
  matrix products  174 us (19%)
  local copies, waits for them, and re-layouts  90.2 us (10%)
  other arithmetic  44.4 us (5%)
  between operations  13.5 us (1%)
    all_gather x1, waiting for transfers between devices, per_device(): lax.all_gather(weight_q, 'text', axis=0, tiled=True)  563 us
    dot_general x8, matrix products, tile_of(): jnp.einsum('tkgd,nkd->kgtn', queries, keys_now, preferred_element_type=jn...  62.6 us
    unnamed x22, local copies, waits for them, and re-layouts  58 us
    dot_general x4, matrix products, backward(): jnp.einsum('kgtn,nkd->kgtd', score_grad, keys_now, preferred_element_type...  48.1 us
    all_gather x1, waiting for transfers between devices, per_device(): lax.all_gather(query_grad, 'text', axis=0, tiled=True)  42.5 us
    dot_general x4, matrix products, forward(): jnp.einsum('kgtn,nkd->kgtd', weights.astype(jnp.bfloat16), values_now, pr...  29.9 us
    reduce_sum x4, other arithmetic, forward(): total = total * fade + jnp.sum(weights, axis=-1)  29.2 us
  transfers between devices with their start and end apart: 3, of which 2 were waited for; matrix products, arithmetic and copies ran while one was open for 24% of the time, Pallas kernels for 0%

commit v1 on v0

--- a/solution.py
+++ b/solution.py
@@ -115,11 +115,8 @@
         jnp.bfloat16
     )
     spread = lax.all_to_all(text_states, "text", split_axis=1, concat_axis=0, tiled=True)
-    q_sum = jnp.dot(
-        text_states,
-        lax.all_gather(weight_q, "text", axis=0, tiled=True),
-        preferred_element_type=jnp.float32,
-    )
+    q_part = jnp.dot(spread, weight_q, preferred_element_type=jnp.float32)
+    q_sum = lax.psum_scatter(q_part, "text", scatter_dimension=0, tiled=True)
     queries = q_sum.astype(jnp.bfloat16)
     first_token = lax.axis_index("text") * tok_dev
     span_ids = (first_token + jnp.arange(tok_dev, dtype=jnp.int32)) // SPAN

time: 937 us -> 433 us (0.46)
  waiting for transfers between devices: 606 us -> 123 us
  other arithmetic: 44.4 us -> 31.7 us
  local copies, waits for them, and re-layouts: 90.2 us -> 79.7 us
    all_gather x1 -> x0, waiting for transfers between devices: 563 us -> none  [per_device(): lax.all_gather(weight_q, 'text', axis=0, tiled=True)]
    reduce_scatter x0 -> x1, waiting for transfers between devices: none -> 57.7 us  [per_device(): q_sum = lax.psum_scatter(q_part, 'text', scatter_dimension=0, tiled=True)]
    all_to_all x1, waiting for transfers between devices: 0.01 us -> 18.3 us  [per_device(): lax.all_to_all(text_states, 'text', split_axis=1, concat_axis=0, tiled=True)]
    convert_element_type x1, other arithmetic: 13.9 us -> 1.28 us  [per_device(): queries = q_sum.astype(jnp.bfloat16)]
    unnamed x22 -> x20, local copies, waits for them, and re-layouts: 58 us -> 51.7 us
  transfers between devices with their start and end apart: 3 -> 3, of which waited for: 2 -> 3; matrix products, arithmetic and copies ran while one was open for 24% -> 11% of each run, Pallas kernels for 0% -> 0%
where the time goes in v1:
time: 433 us; the launch traced here: 431 us
  matrix products  176 us (41%)
  waiting for transfers between devices  123 us (28%)
  local copies, waits for them, and re-layouts  79.7 us (18%)
  other arithmetic  31.7 us (7%)
  between operations  13.5 us (3%)
  starting transfers between devices  6.54 us (2%)
    dot_general x8, matrix products, tile_of(): jnp.einsum('tkgd,nkd->kgtn', queries, keys_now, preferred_element_type=jn...  62.4 us
    reduce_scatter x1, waiting for transfers between devices, per_device(): q_sum = lax.psum_scatter(q_part, 'text', scatter_dimension=0, tiled=True)  57.7 us
    unnamed x20, local copies, waits for them, and re-layouts  51.7 us
    dot_general x4, matrix products, backward(): jnp.einsum('kgtn,nkd->kgtd', score_grad, keys_now, preferred_element_type...  51.7 us
    all_gather x1, waiting for transfers between devices, per_device(): lax.all_gather(query_grad, 'text', axis=0, tiled=True)  46.9 us
    dot_general x4, matrix products, forward(): jnp.einsum('kgtn,nkd->kgtd', weights.astype(jnp.bfloat16), values_now, pr...  29.9 us
    reduce_sum x4, other arithmetic, forward(): total = total * fade + jnp.sum(weights, axis=-1)  29.2 us
    all_to_all x1, waiting for transfers between devices, per_device(): lax.all_to_all(text_states, 'text', split_axis=1, concat_axis=0, tiled=True)  18.3 us
  transfers between devices with their start and end apart: 3, of which 3 were waited for; matrix products, arithmetic and copies ran while one was open for 11% of the time, Pallas kernels for 0%

profile of v1, /device:TPU:0, one launch (start us, length us, event | category | flops | bytes accessed | tf_op | source)
XLA Modules:
  0.0 431.3 jit_solution(5376205303469265212)
XLA Ops:
  6.5 4.1 copy.63
  10.6 6.3 %all-to-all-start = ((bf16[128,4,2048]{0,2,1:T(8,128)(2,1)}), bf16[128,4,2048]{0,2,1:T(8,128)(2,1)S(1)}, u32[]{:S(2)}, u32[]{:S(2)}) async-start(bf16[128,4,2048]{0,2,1:T(8,128)(2,1)} %bitcast.134), calls=%async_computation | async-start | bytes 4194304 | tf_op jit(solution)/shard_map/all_to_all | solution.py:117
  16.9 17.6 %copy.62 = f32[2048,2048]{0,1:T(8,128)} copy(f32[2048,2048]{1,0:T(8,128)} %param.15) | data formatting | bytes 33554432 | tf_op args[2]
  34.5 12.3 %copy.61 = bf16[2048,2048]{0,1:T(8,128)(2,1)} copy(bf16[2048,2048]{1,0:T(8,128)(2,1)} %param.14) | data formatting | bytes 16777216 | tf_op args[1]
  46.8 18.3 %all-to-all-done = bf16[128,4,2048]{0,2,1:T(8,128)(2,1)S(1)} async-done(((bf16[128,4,2048]{0,2,1:T(8,128)(2,1)}), bf16[128,4,2048]{0,2,1:T(8,128)(2,1)S(1)}, u32[]{:S(2)}, u32[]{:S(2)}) %all-to-all-start) | async-done | bytes 2097184 | tf_op jit(solution)/shard_map/all_to_all | solution.py:117
  65.1 2.7 copy.64
  67.8 14.2 %fusion.47 = f32[512,2048]{0,1:T(8,128)} fusion(bf16[512,2048]{1,0:T(8,128)(2,1)} %bitcast.138, bf16[2048,2048]{0,1:T(8,128)(2,1)} %copy.61, f32[2048]{0:T(1024)S(1)} %copy-done.4, f32[2048,2048]{0,1:T(8,128)} %copy.62), kind=kOutput, calls=%fused_computation.54 | convolution fusion | flops 4332716032 | bytes 31465472 | tf_op jit(solution)/shard_map/dot_general | solution.py:118
  82.5 4.3 %copy.65 = bf16[6404,256]{0,1:T(8,128)(2,1)S(1)} copy(bf16[6404,256]{1,0:T(8,128)(2,1)} %param.18) | data formatting | bytes 6557696 | tf_op args[5]
  86.8 3.6 copy.68
  90.5 4.3 copy.60
  94.8 3.6 copy.71
  98.4 1.3 copy.70
  100.3 57.7 %reduce-scatter.2.cloned.1.call-done = f32[128,2048]{0,1:T(8,128)} async-done(((f32[512,2048]{0,1:T(8,128)}), f32[128,2048]{0,1:T(8,128)}) %reduce-scatter.2.cloned.1.call-update) | async-done | bytes 1048592 | tf_op jit(solution)/shard_map/reduce_scatter | solution.py:119
  158.0 1.3 convert_element_type.39
  159.3 0.3 copy.72
  159.6 94.7 %while.32 = (s32[]{:T(128)}, f32[2,8,128]{2,1,0:T(8,128)S(1)}, f32[2,8,128]{2,1,0:T(8,128)S(1)}, f32[2,8,128,128]{3,2,1,0:T(8,128)}, pred[128,4]{0,1:T(4,128)(4,...) while((s32[]{:T(128)}, f32[2,8,128]{2,1,0:T(8,128)S(1)}, ...), condition=%wide.region_8.9_spmd.clone, body=%wide.region_5.8_spmd.clone.sunk | while | flops 1712357376 | bytes 52192112 | solution.py:71
  159.6 7.8 %bitcast_reduce_fusion.2 = (f32[2,8,128]{2,1,0:T(8,128)S(1)}, f32[2,1601,128,8]{2,1,3,0:T(8,128)}) fusion(bf16[128,2,8,128]{3,0,2,1:T(8,128)(2,1)S(1)} %get-tuple-element.659, bf16[6404,2,128]{2,0,1:T(8,128)(2,1)} %get-tuple-element.658, s32[]{:T(128)S(6)} %select_n.117), kind=kOutput, calls=%fused_computation.1.clone.1 | convolution fusion | flops 845940736 | bytes 14471172 | tf_op jit(solution)/shard_map/while/body/eval_jaxpr/tkgd,nkd->kgtn/dot_general | solution.py:41
  167.5 7.3 %fusion.77 = f32[2,8,128]{2,1,0:T(8,128)S(1)} fusion(f32[2,1601,128,8]{2,1,3,0:T(8,128)} %get-tuple-element.616, f32[2,8,128]{2,1,0:T(8,128)S(1)} %maximum_select_fusion.2, pred[128]{0:T(512)(128)(4,1)S(1)} %dynamic-slice_bitcast_fusion.4), kind=kLoop, calls=%fused_computation.5.clone.1 | loop fusion | flops 13113344 | bytes 13131904 | tf_op jit(solution)/shard_map/while/body/eval_jaxpr/reduce_sum | solution.py:57
  174.8 7.5 %fusion.79 = f32[2,8,128,128]{3,2,1,0:T(8,128)S(1)} fusion(f32[2,1601,128,8]{2,1,3,0:T(8,128)} %get-tuple-element.616, f32[2,8,128]{2,1,0:T(8,128)S(1)} %maximum_select_fusion.2, pred[128]{0:T(512)(128)(4,1)S(1)} %dynamic-slice_bitcast_fusion.4, f32[2,8,128,128]{3,2,1,0:T(8,128)S(1)} %copy-done.1, bf16[6404,2,128]{2,0,1:T(8,128)(2,1)} %get-tuple-element.660, ...), kind=kOutput, calls=%fused_computation.8.clone.1 | convolution fusion | flops 853286912 | bytes 16109701 | tf_op jit(solution)/shard_map/while/body/eval_jaxpr/kgtn,nkd->kgtd/dot_general | solution.py:58
  182.3 1.0 copy-done.2
  183.3 7.8 %bitcast_reduce_fusion.2 = (f32[2,8,128]{2,1,0:T(8,128)S(1)}, f32[2,1601,128,8]{2,1,3,0:T(8,128)}) fusion(bf16[128,2,8,128]{3,0,2,1:T(8,128)(2,1)S(1)} %get-tuple-element.659, bf16[6404,2,128]{2,0,1:T(8,128)(2,1)} %get-tuple-element.658, s32[]{:T(128)S(6)} %select_n.117), kind=kOutput, calls=%fused_computation.1.clone.1 | convolution fusion | flops 845940736 | bytes 14471172 | tf_op jit(solution)/shard_map/while/body/eval_jaxpr/tkgd,nkd->kgtn/dot_general | solution.py:41
  191.1 7.3 %fusion.77 = f32[2,8,128]{2,1,0:T(8,128)S(1)} fusion(f32[2,1601,128,8]{2,1,3,0:T(8,128)} %get-tuple-element.616, f32[2,8,128]{2,1,0:T(8,128)S(1)} %maximum_select_fusion.2, pred[128]{0:T(512)(128)(4,1)S(1)} %dynamic-slice_bitcast_fusion.4), kind=kLoop, calls=%fused_computation.5.clone.1 | loop fusion | flops 13113344 | bytes 13131904 | tf_op jit(solution)/shard_map/while/body/eval_jaxpr/reduce_sum | solution.py:57
  198.5 7.5 %fusion.79 = f32[2,8,128,128]{3,2,1,0:T(8,128)S(1)} fusion(f32[2,1601,128,8]{2,1,3,0:T(8,128)} %get-tuple-element.616, f32[2,8,128]{2,1,0:T(8,128)S(1)} %maximum_select_fusion.2, pred[128]{0:T(512)(128)(4,1)S(1)} %dynamic-slice_bitcast_fusion.4, f32[2,8,128,128]{3,2,1,0:T(8,128)S(1)} %copy-done.1, bf16[6404,2,128]{2,0,1:T(8,128)(2,1)} %get-tuple-element.660, ...), kind=kOutput, calls=%fused_computation.8.clone.1 | convolution fusion | flops 853286912 | bytes 16109701 | tf_op jit(solution)/shard_map/while/body/eval_jaxpr/kgtn,nkd->kgtd/dot_general | solution.py:58
  206.0 1.0 copy-done.2
  206.9 7.8 %bitcast_reduce_fusion.2 = (f32[2,8,128]{2,1,0:T(8,128)S(1)}, f32[2,1601,128,8]{2,1,3,0:T(8,128)}) fusion(bf16[128,2,8,128]{3,0,2,1:T(8,128)(2,1)S(1)} %get-tuple-element.659, bf16[6404,2,128]{2,0,1:T(8,128)(2,1)} %get-tuple-element.658, s32[]{:T(128)S(6)} %select_n.117), kind=kOutput, calls=%fused_computation.1.clone.1 | convolution fusion | flops 845940736 | bytes 14471172 | tf_op jit(solution)/shard_map/while/body/eval_jaxpr/tkgd,nkd->kgtn/dot_general | solution.py:41
  214.8 7.3 %fusion.77 = f32[2,8,128]{2,1,0:T(8,128)S(1)} fusion(f32[2,1601,128,8]{2,1,3,0:T(8,128)} %get-tuple-element.616, f32[2,8,128]{2,1,0:T(8,128)S(1)} %maximum_select_fusion.2, pred[128]{0:T(512)(128)(4,1)S(1)} %dynamic-slice_bitcast_fusion.4), kind=kLoop, calls=%fused_computation.5.clone.1 | loop fusion | flops 13113344 | bytes 13131904 | tf_op jit(solution)/shard_map/while/body/eval_jaxpr/reduce_sum | solution.py:57
  222.1 7.5 %fusion.79 = f32[2,8,128,128]{3,2,1,0:T(8,128)S(1)} fusion(f32[2,1601,128,8]{2,1,3,0:T(8,128)} %get-tuple-element.616, f32[2,8,128]{2,1,0:T(8,128)S(1)} %maximum_select_fusion.2, pred[128]{0:T(512)(128)(4,1)S(1)} %dynamic-slice_bitcast_fusion.4, f32[2,8,128,128]{3,2,1,0:T(8,128)S(1)} %copy-done.1, bf16[6404,2,128]{2,0,1:T(8,128)(2,1)} %get-tuple-element.660, ...), kind=kOutput, calls=%fused_computation.8.clone.1 | convolution fusion | flops 853286912 | bytes 16109701 | tf_op jit(solution)/shard_map/while/body/eval_jaxpr/kgtn,nkd->kgtd/dot_general | solution.py:58
  229.6 1.0 copy-done.2
  230.6 7.8 %bitcast_reduce_fusion.2 = (f32[2,8,128]{2,1,0:T(8,128)S(1)}, f32[2,1601,128,8]{2,1,3,0:T(8,128)}) fusion(bf16[128,2,8,128]{3,0,2,1:T(8,128)(2,1)S(1)} %get-tuple-element.659, bf16[6404,2,128]{2,0,1:T(8,128)(2,1)} %get-tuple-element.658, s32[]{:T(128)S(6)} %select_n.117), kind=kOutput, calls=%fused_computation.1.clone.1 | convolution fusion | flops 845940736 | bytes 14471172 | tf_op jit(solution)/shard_map/while/body/eval_jaxpr/tkgd,nkd->kgtn/dot_general | solution.py:41
  238.4 7.3 %fusion.77 = f32[2,8,128]{2,1,0:T(8,128)S(1)} fusion(f32[2,1601,128,8]{2,1,3,0:T(8,128)} %get-tuple-element.616, f32[2,8,128]{2,1,0:T(8,128)S(1)} %maximum_select_fusion.2, pred[128]{0:T(512)(128)(4,1)S(1)} %dynamic-slice_bitcast_fusion.4), kind=kLoop, calls=%fused_computation.5.clone.1 | loop fusion | flops 13113344 | bytes 13131904 | tf_op jit(solution)/shard_map/while/body/eval_jaxpr/reduce_sum | solution.py:57
  245.8 7.5 %fusion.79 = f32[2,8,128,128]{3,2,1,0:T(8,128)S(1)} fusion(f32[2,1601,128,8]{2,1,3,0:T(8,128)} %get-tuple-element.616, f32[2,8,128]{2,1,0:T(8,128)S(1)} %maximum_select_fusion.2, pred[128]{0:T(512)(128)(4,1)S(1)} %dynamic-slice_bitcast_fusion.4, f32[2,8,128,128]{3,2,1,0:T(8,128)S(1)} %copy-done.1, bf16[6404,2,128]{2,0,1:T(8,128)(2,1)} %get-tuple-element.660, ...), kind=kOutput, calls=%fused_computation.8.clone.1 | convolution fusion | flops 853286912 | bytes 16109701 | tf_op jit(solution)/shard_map/while/body/eval_jaxpr/kgtn,nkd->kgtd/dot_general | solution.py:58
  253.3 1.0 copy-done.2
  254.3 1.6 copy.69
  255.8 0.4 multiply_reduce_fusion
  256.2 0.3 copy.74
  256.5 83.1 %while.33 = (s32[]{:T(128)}, f32[2,8,128,128]{3,2,1,0:T(8,128)}, pred[128,4]{0,1:T(4,128)(4,1)S(1)}, bf16[6404,2,128]{2,0,1:T(8,128)(2,1)}, bf16[128,2,8,128]{3,...) while((s32[]{:T(128)}, f32[2,8,128,128]{3,2,1,0:T(8,128)}, ...), condition=%wide.region_11.12_spmd.clone, body=%wide.region_10.11_spmd.clone.sunk | while | flops 2544910336 | bytes 31930436 | solution.py:92
  256.7 7.9 %fusion.85 = f32[2,1601,128,8]{2,1,3,0:T(8,128)} fusion(bf16[128,2,8,128]{3,0,2,1:T(8,128)(2,1)S(1)} %get-tuple-element.697, bf16[6404,2,128]{2,0,1:T(8,128)(2,1)} %get-tuple-element.696, s32[]{:T(128)S(6)} %select_n.119), kind=kOutput, calls=%fused_computation.35.clone.1 | convolution fusion | flops 839385088 | bytes 14462980 | tf_op jit(solution)/shard_map/while/body/eval_jaxpr/tkgd,nkd->kgtn/dot_general | solution.py:41
  264.6 12.7 %fusion.86 = f32[2,8,128,128]{3,2,1,0:T(8,128)} fusion(f32[2,1601,128,8]{2,1,3,0:T(8,128)} %fusion.85, bf16[2,8,128,128]{3,2,1,0:T(8,128)(2,1)S(1)} %get-tuple-element.701, f32[2,8,128]{2,1,0:T(8,128)S(1)} %get-tuple-element.702, f32[2,8,128]{2,1,0:T(8,128)S(1)} %get-tuple-element.699, f32[2,8,128]{2,1,0:T(8,128)S(1)} %get-tuple-element.698, ...), kind=kOutput, calls=%fused_computation.32.clone.1 | convolution fusion | flops 1705525248 | bytes 17467008 | tf_op jit(solution)/shard_map/while/body/eval_jaxpr/kgtn,nkd->kgtd/dot_general | solution.py:88
  277.3 7.7 %fusion.85 = f32[2,1601,128,8]{2,1,3,0:T(8,128)} fusion(bf16[128,2,8,128]{3,0,2,1:T(8,128)(2,1)S(1)} %get-tuple-element.697, bf16[6404,2,128]{2,0,1:T(8,128)(2,1)} %get-tuple-element.696, s32[]{:T(128)S(6)} %select_n.119), kind=kOutput, calls=%fused_computation.35.clone.1 | convolution fusion | flops 839385088 | bytes 14462980 | tf_op jit(solution)/shard_map/while/body/eval_jaxpr/tkgd,nkd->kgtn/dot_general | solution.py:41
  285.1 13.0 %fusion.86 = f32[2,8,128,128]{3,2,1,0:T(8,128)} fusion(f32[2,1601,128,8]{2,1,3,0:T(8,128)} %fusion.85, bf16[2,8,128,128]{3,2,1,0:T(8,128)(2,1)S(1)} %get-tuple-element.701, f32[2,8,128]{2,1,0:T(8,128)S(1)} %get-tuple-element.702, f32[2,8,128]{2,1,0:T(8,128)S(1)} %get-tuple-element.699, f32[2,8,128]{2,1,0:T(8,128)S(1)} %get-tuple-element.698, ...), kind=kOutput, calls=%fused_computation.32.clone.1 | convolution fusion | flops 1705525248 | bytes 17467008 | tf_op jit(solution)/shard_map/while/body/eval_jaxpr/kgtn,nkd->kgtd/dot_general | solution.py:88
  298.1 7.7 %fusion.85 = f32[2,1601,128,8]{2,1,3,0:T(8,128)} fusion(bf16[128,2,8,128]{3,0,2,1:T(8,128)(2,1)S(1)} %get-tuple-element.697, bf16[6404,2,128]{2,0,1:T(8,128)(2,1)} %get-tuple-element.696, s32[]{:T(128)S(6)} %select_n.119), kind=kOutput, calls=%fused_computation.35.clone.1 | convolution fusion | flops 839385088 | bytes 14462980 | tf_op jit(solution)/shard_map/while/body/eval_jaxpr/tkgd,nkd->kgtn/dot_general | solution.py:41
  305.8 13.0 %fusion.86 = f32[2,8,128,128]{3,2,1,0:T(8,128)} fusion(f32[2,1601,128,8]{2,1,3,0:T(8,128)} %fusion.85, bf16[2,8,128,128]{3,2,1,0:T(8,128)(2,1)S(1)} %get-tuple-element.701, f32[2,8,128]{2,1,0:T(8,128)S(1)} %get-tuple-element.702, f32[2,8,128]{2,1,0:T(8,128)S(1)} %get-tuple-element.699, f32[2,8,128]{2,1,0:T(8,128)S(1)} %get-tuple-element.698, ...), kind=kOutput, calls=%fused_computation.32.clone.1 | convolution fusion | flops 1705525248 | bytes 17467008 | tf_op jit(solution)/shard_map/while/body/eval_jaxpr/kgtn,nkd->kgtd/dot_general | solution.py:88
  318.8 7.7 %fusion.85 = f32[2,1601,128,8]{2,1,3,0:T(8,128)} fusion(bf16[128,2,8,128]{3,0,2,1:T(8,128)(2,1)S(1)} %get-tuple-element.697, bf16[6404,2,128]{2,0,1:T(8,128)(2,1)} %get-tuple-element.696, s32[]{:T(128)S(6)} %select_n.119), kind=kOutput, calls=%fused_computation.35.clone.1 | convolution fusion | flops 839385088 | bytes 14462980 | tf_op jit(solution)/shard_map/while/body/eval_jaxpr/tkgd,nkd->kgtn/dot_general | solution.py:41
  326.6 13.0 %fusion.86 = f32[2,8,128,128]{3,2,1,0:T(8,128)} fusion(f32[2,1601,128,8]{2,1,3,0:T(8,128)} %fusion.85, bf16[2,8,128,128]{3,2,1,0:T(8,128)(2,1)S(1)} %get-tuple-element.701, f32[2,8,128]{2,1,0:T(8,128)S(1)} %get-tuple-element.702, f32[2,8,128]{2,1,0:T(8,128)S(1)} %get-tuple-element.699, f32[2,8,128]{2,1,0:T(8,128)S(1)} %get-tuple-element.698, ...), kind=kOutput, calls=%fused_computation.32.clone.1 | convolution fusion | flops 1705525248 | bytes 17467008 | tf_op jit(solution)/shard_map/while/body/eval_jaxpr/kgtn,nkd->kgtd/dot_general | solution.py:88
  339.6 2.2 copy.75
  341.8 46.9 %all-gather.2.cloned.1.call-done = bf16[512,2048]{0,1:T(8,128)(2,1)} async-done(((bf16[128,2048]{0,1:T(8,128)(2,1)}), bf16[512,2048]{0,1:T(8,128)(2,1)}) %all-gather.2.cloned.1.call-update) | async-done | bytes 2097168 | tf_op jit(solution)/shard_map/all_gather | solution.py:136
  388.7 18.2 %fusion.42 = f32[2048,2048]{0,1:T(8,128)} fusion(bf16[512,2048]{0,1:T(8,128)(2,1)} %all-gather.2.cloned.1.call-done, bf16[512,2048]{1,0:T(8,128)(2,1)S(1)} %bitcast.139, f32[2048]{0:T(1024)S(1)} %copy-done.5, f32[2048,2048]{0,1:T(8,128)} %copy.62), kind=kOutput, calls=%fused_computation.47 | convolution fusion | flops 4357881856 | bytes 37756928 | tf_op jit(solution)/shard_map/dot_general | solution.py:134
  406.9 17.6 %copy.76 = f32[2048,2048]{1,0:T(8,128)} copy(f32[2048,2048]{0,1:T(8,128)} %fusion.42) | data formatting | bytes 33554432 | tf_op jit(solution)/shard_map/mul | solution.py:142
  (58 shorter events, 1.2 us)
Async XLA Ops:
  10.6 54.5 %all-to-all-start = ((bf16[128,4,2048]{0,2,1:T(8,128)(2,1)}), bf16[128,4,2048]{0,2,1:T(8,128)(2,1)S(1)}, u32[]{:S(2)}, u32[]{:S(2)}) async-start(bf16[128,4,2048]{0,2,1:T(8,128)(2,1)} %bitcast.134), calls=%async_computation | async-start | bytes 4194304 | tf_op jit(solution)/shard_map/all_to_all | solution.py:117
  16.9 141.1 %reduce-scatter.2.cloned.1.call-start = ((), (), s32[]{:S(2)}) async-start(), calls=%async_computation.2 | async-start | bytes 5242880 | tf_op jit(solution)/shard_map/reduce_scatter | solution.py:119
  34.5 33.3 %copy-start.4 = (f32[2048]{0:T(1024)S(1)}, f32[2048]{0:T(1024)}, u32[]{:S(2)}) copy-start(f32[2048]{0:T(1024)} %param.16) | copy-start | bytes 24580
  67.8 14.5 %copy-start.6 = (s32[3]{0:T(128)S(1)}, s32[3]{0:T(128)}, u32[]{:S(2)}) copy-start(s32[3]{0:T(128)} %param.20) | copy-start | bytes 40
  82.0 306.7 %all-gather.2.cloned.1.call-start = ((), (), s32[]{:S(2)}) async-start(), calls=%async_computation.3 | async-start | bytes 2621440 | tf_op jit(solution)/shard_map/all_gather | solution.py:136
  82.5 17.5 %copy-start.3 = (s32[4]{0:T(128)S(1)}, s32[4]{0:T(128)}, u32[]{:S(2)}) copy-start(s32[4]{0:T(128)} %param.21) | copy-start | bytes 52
  159.6 15.2 %copy-start.1 = (f32[2,8,128,128]{3,2,1,0:T(8,128)S(1)}, f32[2,8,128,128]{3,2,1,0:T(8,128)}, u32[]{:S(2)}) copy-start(f32[2,8,128,128]{3,2,1,0:T(8,128)} %get-tuple-element.644) | copy-start | bytes 3145732 | tf_op jit(solution)/shard_map/while
  182.3 1.0 copy-start.2
  183.3 15.2 %copy-start.1 = (f32[2,8,128,128]{3,2,1,0:T(8,128)S(1)}, f32[2,8,128,128]{3,2,1,0:T(8,128)}, u32[]{:S(2)}) copy-start(f32[2,8,128,128]{3,2,1,0:T(8,128)} %get-tuple-element.644) | copy-start | bytes 3145732 | tf_op jit(solution)/shard_map/while
  205.9 1.0 copy-start.2
  206.9 15.2 %copy-start.1 = (f32[2,8,128,128]{3,2,1,0:T(8,128)S(1)}, f32[2,8,128,128]{3,2,1,0:T(8,128)}, u32[]{:S(2)}) copy-start(f32[2,8,128,128]{3,2,1,0:T(8,128)} %get-tuple-element.644) | copy-start | bytes 3145732 | tf_op jit(solution)/shard_map/while
  229.6 1.0 copy-start.2
  230.6 15.2 %copy-start.1 = (f32[2,8,128,128]{3,2,1,0:T(8,128)S(1)}, f32[2,8,128,128]{3,2,1,0:T(8,128)}, u32[]{:S(2)}) copy-start(f32[2,8,128,128]{3,2,1,0:T(8,128)} %get-tuple-element.644) | copy-start | bytes 3145732 | tf_op jit(solution)/shard_map/while
  253.3 1.0 copy-start.2
  256.5 132.2 %copy-start = (bf16[4,128,2048]{2,1,0:T(8,128)(2,1)S(1)}, bf16[4,128,2048]{2,1,0:T(8,128)(2,1)}, u32[]{:S(2)}) copy-start(bf16[4,128,2048]{2,1,0:T(8,128)(2,1)} %copy.64) | copy-start | bytes 6291460
  256.5 132.2 %copy-start.5 = (f32[2048]{0:T(1024)S(1)}, f32[2048]{0:T(1024)}, u32[]{:S(2)}) copy-start(f32[2048]{0:T(1024)} %param.16) | copy-start | bytes 24580
Sparse Core Ops, SparseCore 0:
  82.2 75.8 reduce-scatter.1
  341.9 46.7 all-gather.1

commit v2 on v1

v2 whole, which is shorter than its diff:
```python
import functools

import jax
import jax.numpy as jnp
from jax import lax
from jax.experimental import pallas as pl
from jax.experimental.pallas import tpu as pltpu
from jax.sharding import PartitionSpec as P

H = 64
KVH = 8
HD = 128
IMG_TOK = 1601
SPAN = 128
MAX_SEEN = 2
KEYS = MAX_SEEN * IMG_TOK
KEYS_PAD = -(-KEYS // 256) * 256
CHUNKS = 2
NEG = -1e30


def visibility(span_ids, doc_images, image_start, total_spans):
    images = image_start.shape[0]
    documents = doc_images.shape[0]
    doc_ends = jnp.cumsum(doc_images)
    positions = jnp.arange(images, dtype=jnp.int32)
    doc_of = jnp.sum((positions[:, None] >= doc_ends[None, :]).astype(jnp.int32), axis=1)
    doc_index = jnp.arange(documents, dtype=jnp.int32)
    end_of = jnp.sum(jnp.where(doc_index[None, :] == doc_of[:, None], doc_ends[None, :], 0), axis=1)
    stop_at = jnp.sum(
        jnp.where(positions[None, :] == end_of[:, None], image_start[None, :], 0), axis=1
    )
    stop_at = stop_at + jnp.where(end_of >= images, total_spans, 0)
    return (span_ids[:, None] >= image_start[None, :]) & (span_ids[:, None] < stop_at[None, :])


NT = (((1,), (1,)), ((), ()))


def attention_kernel(bounds_ref, q_ref, k_ref, v_ref, t_ref, o_ref):
    first = bounds_ref[0]
    stop = bounds_ref[1]
    scaling = HD ** (-0.5)
    tokens, width = q_ref.shape
    heads = width // HD

    def stacked(ref):
        return jnp.concatenate([ref[:, h * HD : (h + 1) * HD] for h in range(heads)], axis=0)

    @pl.when(stop <= first)
    def _():
        o_ref[...] = jnp.zeros_like(o_ref)

    @pl.when(stop > first)
    def _():
        row = lax.broadcasted_iota(jnp.int32, (1, KEYS_PAD), 1)
        bias = jnp.where((row >= first) & (row < stop), 0.0, NEG)
        q = stacked(q_ref).astype(jnp.bfloat16)
        k = k_ref[...]
        v = v_ref[...]
        s = lax.dot_general(q, k, NT, preferred_element_type=jnp.float32) * scaling + bias
        peak = jnp.max(s, axis=-1, keepdims=True)
        w = jnp.exp(s - peak)
        total = jnp.sum(w, axis=-1, keepdims=True)
        acc = jnp.dot(w.astype(jnp.bfloat16), v, preferred_element_type=jnp.float32)
        inv = 1.0 / jnp.maximum(total, 1.0)
        attended = acc * inv
        out_grad = (1024.0 * (attended - stacked(t_ref).astype(jnp.float32))).astype(jnp.bfloat16)
        delta = jnp.sum(out_grad.astype(jnp.float32) * attended, axis=-1, keepdims=True)
        dp = lax.dot_general(out_grad, v, NT, preferred_element_type=jnp.float32)
        ds = (w * ((dp - delta) * (inv * scaling))).astype(jnp.bfloat16)
        g = jnp.dot(ds, k, preferred_element_type=jnp.float32).astype(o_ref.dtype)
        for h in range(heads):
            o_ref[:, h * HD : (h + 1) * HD] = g[h * tokens : (h + 1) * tokens]


def attention(bounds, queries, keys, values, target, chunk):
    tokens, width = queries.shape
    pair = 2 * HD
    steps = width // pair
    group = (H // KVH) * HD
    base = chunk * steps

    def kv_map(i, b):
        return (0, ((base + i) * pair) // group)

    return pl.pallas_call(
        attention_kernel,
        out_shape=jax.ShapeDtypeStruct((tokens, width), jnp.bfloat16),
        grid_spec=pltpu.PrefetchScalarGridSpec(
            num_scalar_prefetch=1,
            grid=(steps,),
            in_specs=[
                pl.BlockSpec((tokens, pair), lambda i, b: (0, i)),
                pl.BlockSpec((KEYS_PAD, HD), kv_map),
                pl.BlockSpec((KEYS_PAD, HD), kv_map),
                pl.BlockSpec((tokens, pair), lambda i, b: (0, base + i)),
            ],
            out_specs=pl.BlockSpec((tokens, pair), lambda i, b: (0, i)),
        ),
        compiler_params=pltpu.CompilerParams(vmem_limit_bytes=44 << 20),
        cost_estimate=pl.CostEstimate(
            flops=20 * tokens * width * KEYS_PAD // 2,
            bytes_accessed=4 * KEYS_PAD * HD + 8 * tokens * width,
            transcendentals=tokens * (width // HD) * KEYS_PAD,
        ),
        name="attention",
    )(bounds, queries, keys, values, target)


def final_kernel(x_ref, g_ref, r_ref, c_ref, *rest):
    o_ref = rest[-1]
    wg = jnp.dot(x_ref[...], g_ref[...], preferred_element_type=jnp.float32)
    t = jnp.tanh(0.5 * r_ref[...])
    t2 = t * t
    o_ref[...] = (wg * (0.3 * c_ref[...]) - (4.0 * 1.728 * 0.3) * (t2 * t)) * (1.0 - t2)


def final(spread_t, grad, logits, steps, previous, chunk):
    rows, tokens = spread_t.shape
    width = grad.shape[1]
    tm = 256
    in_specs = [
        pl.BlockSpec((tm, tokens), lambda i: (i, 0)),
        pl.BlockSpec((tokens, width), lambda i: (0, 0)),
        pl.BlockSpec((tm, width), lambda i: (i, chunk)),
        pl.BlockSpec((1, width), lambda i: (0, chunk)),
    ]
    args = [spread_t, grad, logits, steps]
    aliases = {}
    if previous is not None:
        in_specs.append(pl.BlockSpec(memory_space=pl.ANY))
        args.append(previous)
        aliases = {4: 0}
    return pl.pallas_call(
        final_kernel,
        out_shape=jax.ShapeDtypeStruct(logits.shape, jnp.float32),
        grid=(rows // tm,),
        in_specs=in_specs,
        out_specs=pl.BlockSpec((tm, width), lambda i: (i, chunk)),
        input_output_aliases=aliases,
        compiler_params=pltpu.CompilerParams(vmem_limit_bytes=40 << 20),
        cost_estimate=pl.CostEstimate(
            flops=2 * rows * tokens * width,
            bytes_accessed=8 * rows * width + 2 * tokens * (rows + width),
            transcendentals=rows * width,
        ),
        name="final",
    )(*args)


def per_device(
    text_states,
    grid_levels,
    round_logits,
    column_steps,
    image_keys,
    image_values,
    target_out,
    doc_images,
    image_start,
):
    tok_dev = text_states.shape[0]
    out_cols = grid_levels.shape[1]
    n_text = lax.axis_size("text")
    assert tok_dev == SPAN
    images = image_start.shape[0]
    steps_row = column_steps[None, :]

    spread = lax.all_to_all(text_states, "text", split_axis=1, concat_axis=0, tiled=True)
    soft = 0.5 + 0.6 * jnp.tanh(0.5 * round_logits)
    weight_q = (steps_row * (grid_levels.astype(jnp.float32) + soft)).astype(jnp.bfloat16)
    weight_q = lax.optimization_barrier(weight_q)

    span_ids = jnp.reshape(lax.axis_index("text"), (1,)).astype(jnp.int32)
    visible = visibility(span_ids, doc_images, image_start, n_text)[0]
    seen_before = jnp.cumsum(visible.astype(jnp.int32))
    count = seen_before[-1]
    lowest = jnp.sum((seen_before == 0).astype(jnp.int32))
    base = jnp.minimum(lowest, images - MAX_SEEN)
    first = (lowest - base) * IMG_TOK
    bounds = jnp.stack([first, first + count * IMG_TOK]).astype(jnp.int32)

    def window(array):
        rows = lax.dynamic_slice_in_dim(array, base * IMG_TOK, KEYS, 0)
        return jnp.pad(rows, ((0, KEYS_PAD - KEYS), (0, 0)))

    keys = window(image_keys)
    values = window(image_values)

    width = out_cols // CHUNKS
    grads = []
    sums = []
    for c in range(CHUNKS):
        part = jnp.dot(
            spread, weight_q[:, c * width : (c + 1) * width], preferred_element_type=jnp.float32
        )
        sums.append(lax.psum_scatter(part, "text", scatter_dimension=0, tiled=True))
    for c in range(CHUNKS):
        local = attention(bounds, sums[c], keys, values, target_out, c)
        grads.append(lax.all_gather(local, "text", axis=0, tiled=True))
    spread_t = spread.T
    result = None
    for c in range(CHUNKS):
        result = final(spread_t, grads[c], round_logits, steps_row, result, c)
    return result


def solution(mesh):
    placed = (
        P(("groups", "text"), None),
        P(("groups", "text"), "image"),
        P(("groups", "text"), "image"),
        P(("groups", "image")),
        P("groups", "image"),
        P("groups", "image"),
        P(("groups", "text"), "image"),
        P("groups"),
        P("groups"),
    )
    return jax.shard_map(
        per_device,
        mesh=mesh,
        in_specs=placed,
        out_specs=P(("groups", "text"), "image"),
        check_vma=False,
    )
```

time: 433 us -> 238 us (0.55)
  matrix products: 176 us -> 12.6 us
  local copies, waits for them, and re-layouts: 79.7 us -> 17.4 us
  waiting for transfers between devices: 123 us -> 147 us
  Pallas kernels: 0 us -> 23.9 us
  other arithmetic: 31.7 us -> 14.1 us
    dot_general x18 -> x2, matrix products: 176 us -> 12.6 us  [per_device(): jnp.dot(spread, weight_q[:, c * width:(c + 1) * width], preferred_element...]
    unnamed x20 -> x25, local copies, waits for them, and re-layouts: 51.7 us -> 12.1 us
    reduce_sum x5 -> x1, other arithmetic: 29.6 us -> 0.63 us  [per_device(): lowest = jnp.sum((seen_before == 0).astype(jnp.int32))]
    pallas_call x0 -> x4, Pallas kernels: none -> 23.9 us  [the longest x2 21.6 us: final(): pl.pallas_call(final_kernel, out_shape=jax.ShapeDtypeStruct(logits.shape,...]
    mul x1 -> x0, local copies, waits for them, and re-layouts: 17.6 us -> none  [per_device(): (weight_grad * column_steps[None, :] - 4.0 * centered * centered * center...]
    all_to_all x1, waiting for transfers between devices: 18.3 us -> 35.6 us  [per_device(): lax.all_to_all(text_states, 'text', split_axis=1, concat_axis=0, tiled=True)]
    reduce_scatter x1 -> x2, waiting for transfers between devices: 57.7 us -> 71.3 us  [per_device(): sums.append(lax.psum_scatter(part, 'text', scatter_dimension=0, tiled=True))]
    convert_element_type x1 -> x2, other arithmetic: 1.28 us -> 12.6 us  [the longest x1 12.6 us: per_device(): (steps_row * (grid_levels.astype(jnp.float32) + soft)).astype(jnp.bfloat16)]
  transfers between devices with their start and end apart: 3 -> 5, of which waited for: 3 -> 5; matrix products, arithmetic and copies ran while one was open for 11% -> 11% of each run, Pallas kernels for 0% -> 6%
where the time goes in v2:
time: 238 us; the launch traced here: 237 us
  waiting for transfers between devices  147 us (62%)
  Pallas kernels  23.9 us (10%)
  local copies, waits for them, and re-layouts  17.4 us (7%)
  between operations  15.2 us (6%)
  other arithmetic  14.1 us (6%)
  matrix products  12.6 us (5%)
  starting transfers between devices  6.63 us (3%)
    reduce_scatter x2, waiting for transfers between devices, per_device(): sums.append(lax.psum_scatter(part, 'text', scatter_dimension=0, tiled=True))  71.3 us
    all_gather x2, waiting for transfers between devices, per_device(): grads.append(lax.all_gather(local, 'text', axis=0, tiled=True))  39.9 us
    all_to_all x1, waiting for transfers between devices, per_device(): lax.all_to_all(text_states, 'text', split_axis=1, concat_axis=0, tiled=True)  35.6 us
    pallas_call x2, Pallas kernels, final(): pl.pallas_call(final_kernel, out_shape=jax.ShapeDtypeStruct(logits.shape,...  21.6 us
    convert_element_type x1, other arithmetic, per_device(): (steps_row * (grid_levels.astype(jnp.float32) + soft)).astype(jnp.bfloat16)  12.6 us
    dot_general x2, matrix products, per_device(): jnp.dot(spread, weight_q[:, c * width:(c + 1) * width], preferred_element...  12.6 us
    unnamed x25, local copies, waits for them, and re-layouts  12.1 us
    all_to_all x1, starting transfers between devices, per_device(): lax.all_to_all(text_states, 'text', split_axis=1, concat_axis=0, tiled=True)  6.32 us
  transfers between devices with their start and end apart: 5, of which 5 were waited for; matrix products, arithmetic and copies ran while one was open for 11% of the time, Pallas kernels for 6%

profile of v2, /device:TPU:0, one launch (start us, length us, event | category | flops | bytes accessed | tf_op | source)
XLA Modules:
  0.0 236.7 jit_solution(14764419589794232086)
XLA Ops:
  6.5 4.1 %copy.18 = bf16[128,8192]{0,1:T(8,128)(2,1)} copy(bf16[128,8192]{1,0:T(8,128)(2,1)} %param.9) | data formatting | bytes 4194304 | tf_op args[0]
  10.6 6.3 %all-to-all-start = ((bf16[128,4,2048]{0,2,1:T(8,128)(2,1)}), bf16[128,4,2048]{0,2,1:T(8,128)(2,1)S(1)}, u32[]{:S(2)}, u32[]{:S(2)}) async-start(bf16[128,4,2048]{0,2,1:T(8,128)(2,1)} %bitcast.37), calls=%async_computation | async-start | bytes 4194304 | tf_op jit(solution)/shard_map/all_to_all | solution.py:170
  16.9 0.0 reduce-scatter.5.cloned.1.call-start
  16.9 0.0 copy-done.4
  16.9 12.6 %multiply_convert_fusion = bf16[2048,2048]{1,0:T(8,128)(2,1)} fusion(f32[2048,2048]{1,0:T(8,128)} %r_ref.3, bf16[2048,2048]{1,0:T(8,128)(2,1)} %param.10, f32[2048]{0:T(1024)S(1)} %copy-done.4), kind=kLoop, calls=%fused_computation | loop fusion | flops 29360128 | bytes 33562624 | tf_op jit(solution)/shard_map/convert_element_type | solution.py:172
  29.5 35.6 %all-to-all-done = bf16[128,4,2048]{0,2,1:T(8,128)(2,1)S(1)} async-done(((bf16[128,4,2048]{0,2,1:T(8,128)(2,1)}), bf16[128,4,2048]{0,2,1:T(8,128)(2,1)S(1)}, u32[]{:S(2)}, u32[]{:S(2)}) %all-to-all-start) | async-done | bytes 2097184 | tf_op jit(solution)/shard_map/all_to_all | solution.py:170
  65.1 6.7 %fusion.11 = f32[512,1024]{1,0:T(8,128)} fusion(bf16[2048,2048]{1,0:T(8,128)(2,1)} %multiply_convert_fusion, bf16[128,4,2048]{0,2,1:T(8,128)(2,1)S(1)} %all-to-all-done), kind=kOutput, calls=%fused_computation.9 | convolution fusion | flops 2147483648 | bytes 8388608 | tf_op jit(solution)/shard_map/dot_general | solution.py:195
  71.8 0.0 reduce-scatter.5.cloned.1.call-update
  71.8 0.0 copy-start.11
  71.8 0.0 copy-start.10
  71.8 0.0 reduce-scatter.3.cloned.1.call-start
  71.9 0.0 copy-done.9
  71.9 5.9 %fusion.6 = f32[512,1024]{1,0:T(8,128)} fusion(bf16[2048,2048]{1,0:T(8,128)(2,1)} %multiply_convert_fusion, bf16[128,4,2048]{0,2,1:T(8,128)(2,1)S(1)} %all-to-all-done), kind=kOutput, calls=%fused_computation.8 | convolution fusion | flops 2147483648 | bytes 8388608 | tf_op jit(solution)/shard_map/dot_general | solution.py:195
  77.8 0.0 reduce-scatter.3.cloned.1.call-update
  77.8 0.0 all-gather.5.cloned.1.call-start
  77.9 0.0 copy-done.11
  77.9 0.2 reduce-window.13
  78.1 0.1 convert_reduce_fusion
  78.2 0.2 select_reduce_fusion.1
  78.4 0.2 select_reduce_fusion
  78.6 0.2 reduce-window.14
  78.8 0.6 slice.10
  79.4 0.6 fusion.19
  81.3 2.7 %constant_dynamic-slice_fusion = (bf16[3202,256]{1,0:T(8,128)(2,1)S(1)}, bf16[3202,256]{1,0:T(8,128)(2,1)S(1)}) fusion(bf16[6404,256]{1,0:T(8,128)(2,1)} %param.13, s32[]{:T(128)S(6)} %select_n.19, bf16[6404,256]{1,0:T(8,128)(2,1)} %param.14), kind=kLoop, calls=%fused_computation.24 | loop fusion | bytes 6557700 | tf_op jit(solution)/shard_map/dynamic_slice | solution.py:185
  84.0 0.1 pad.7.k_ref
  84.1 0.1 pad.8.v_ref
  84.9 0.1 pad_add_fusion.bounds_ref
  84.9 29.7 %reduce-scatter.5.cloned.1.call-done.q_ref = f32[128,1024]{1,0:T(8,128)} async-done(((f32[512,1024]{1,0:T(8,128)}), f32[128,1024]{1,0:T(8,128)}) %reduce-scatter.5.cloned.1.call-update) | async-done | bytes 524304 | tf_op jit(solution)/shard_map/reduce_scatter | solution.py:198
  114.6 1.0 copy-done.5
  115.7 1.0 copy-done.8
  116.7 1.2 attention.3
  117.9 0.0 copy-start.2
  117.9 0.7 copy-done.2
  118.6 0.0 all-gather.5.cloned.1.call-update
  118.6 0.2 all-gather.3.cloned.1.call-start
  118.9 41.6 %reduce-scatter.3.cloned.1.call-done.q_ref = f32[128,1024]{1,0:T(8,128)} async-done(((f32[512,1024]{1,0:T(8,128)}), f32[128,1024]{1,0:T(8,128)}) %reduce-scatter.3.cloned.1.call-update) | async-done | bytes 524304 | tf_op jit(solution)/shard_map/reduce_scatter | solution.py:198
  160.5 1.0 copy-done.6
  161.5 1.0 copy-done.7
  162.6 1.2 attention.2
  163.8 0.7 copy-done.3
  164.4 0.0 all-gather.3.cloned.1.call-update
  164.5 1.8 bitcast_bitcast_fusion.x_ref
  166.3 23.0 %all-gather.5.cloned.1.call-done.g_ref = bf16[512,1024]{1,0:T(8,128)(2,1)} async-done(((bf16[128,1024]{1,0:T(8,128)(2,1)}), bf16[512,1024]{1,0:T(8,128)(2,1)}) %all-gather.5.cloned.1.call-update) | async-done | bytes 1048592 | tf_op jit(solution)/shard_map/all_gather | solution.py:201
  189.2 1.2 copy-done
  190.5 10.8 %final.2.rest_0_ = f32[2048,2048]{1,0:T(8,128)} custom-call(bf16[2048,512]{1,0:T(8,128)(2,1)S(1)} %bitcast_bitcast_fusion.x_ref, bf16[512,1024]{1,0:T(8,128)(2,1)S(1)} %copy-done, f32[2048,2048]{1,0:T(8,128)} %r_ref.3, f32[1,2048]{1,0:T(1,128)S(1)} %bitcast.35), custom_call_target="tpu_custom_call" | custom-call | flops 2147483648 | bytes 19922944 | tf_op jit(solution)/shard_map/final/pallas_call | solution.py:135
  201.3 16.9 %all-gather.3.cloned.1.call-done.g_ref = bf16[512,1024]{1,0:T(8,128)(2,1)} async-done(((bf16[128,1024]{1,0:T(8,128)(2,1)}), bf16[512,1024]{1,0:T(8,128)(2,1)}) %all-gather.3.cloned.1.call-update) | async-done | bytes 1048592 | tf_op jit(solution)/shard_map/all_gather | solution.py:201
  218.2 1.2 copy-done.1
  219.4 10.8 %final.3 = f32[2048,2048]{1,0:T(8,128)} custom-call(bf16[2048,512]{1,0:T(8,128)(2,1)S(1)} %bitcast_bitcast_fusion.x_ref, bf16[512,1024]{1,0:T(8,128)(2,1)S(1)} %copy-done.1, f32[2048,2048]{1,0:T(8,128)} %r_ref.3, f32[1,2048]{1,0:T(1,128)S(1)} %bitcast.36, f32[2048,2048]{1,0:T(8,128)} %final.2.rest_0_), custom_call_target="tpu_custom_call", output_to_operand_aliasing={{}: (4, {})} | custom-call | flops 2147483648 | bytes 19922944 | tf_op jit(solution)/shard_map/final/pallas_call | solution.py:135
  (11 shorter events, 0.0 us)
Async XLA Ops:
  6.5 10.4 %copy-start.4 = (f32[2048]{0:T(1024)S(1)}, f32[2048]{0:T(1024)}, u32[]{:S(2)}) copy-start(f32[2048]{0:T(1024)} %param.12) | copy-start | bytes 24580
  10.6 54.5 %all-to-all-start = ((bf16[128,4,2048]{0,2,1:T(8,128)(2,1)}), bf16[128,4,2048]{0,2,1:T(8,128)(2,1)S(1)}, u32[]{:S(2)}, u32[]{:S(2)}) async-start(bf16[128,4,2048]{0,2,1:T(8,128)(2,1)} %bitcast.37), calls=%async_computation | async-start | bytes 4194304 | tf_op jit(solution)/shard_map/all_to_all | solution.py:170
  16.9 97.7 %reduce-scatter.5.cloned.1.call-start = ((), (), s32[]{:S(2)}) async-start(), calls=%async_computation.5 | async-start | bytes 2621440 | tf_op jit(solution)/shard_map/reduce_scatter | solution.py:198
  65.1 6.8 %copy-start.9 = (bf16[128,4,2048]{0,2,1:T(8,128)(2,1)}, bf16[128,4,2048]{0,2,1:T(8,128)(2,1)S(1)}, u32[]{:S(2)}) copy-start(bf16[128,4,2048]{0,2,1:T(8,128)(2,1)S(1)} %all-to-all-done) | copy-start | bytes 6291460
  71.8 6.1 %copy-start.11 = (s32[3]{0:T(128)S(1)}, s32[3]{0:T(128)}, u32[]{:S(2)}) copy-start(s32[3]{0:T(128)} %param.16) | copy-start | bytes 40
  71.8 6.6 %copy-start.10 = (s32[4]{0:T(128)S(1)}, s32[4]{0:T(128)}, u32[]{:S(2)}) copy-start(s32[4]{0:T(128)} %param.17) | copy-start | bytes 52
  71.8 88.6 %reduce-scatter.3.cloned.1.call-start = ((), (), s32[]{:S(2)}) async-start(), calls=%async_computation.3 | async-start | bytes 2621440 | tf_op jit(solution)/shard_map/reduce_scatter | solution.py:198
  77.8 111.4 %all-gather.5.cloned.1.call-start = ((), (), s32[]{:S(2)}) async-start(), calls=%async_computation.6 | async-start | bytes 1310720 | tf_op jit(solution)/shard_map/all_gather | solution.py:201
  114.6 1.0 copy-start.5
  115.7 1.0 copy-start.8
  117.9 0.7 copy-start.2
  118.6 99.6 %all-gather.3.cloned.1.call-start = ((), (), s32[]{:S(2)}) async-start(), calls=%async_computation.4 | async-start | bytes 1310720 | tf_op jit(solution)/shard_map/all_gather | solution.py:201
  160.5 1.0 copy-start.6
  161.5 1.0 copy-start.7
  163.8 0.7 copy-start.3
  189.2 1.2 copy-start
  218.2 1.2 copy-start.1
Sparse Core Ops, SparseCore 0:
  71.9 42.6 reduce-scatter.4
  117.0 43.3 reduce-scatter.2
  162.0 27.1 all-gather.4
  190.7 27.4 all-gather.2

commit v3 on v2

--- a/solution.py
+++ b/solution.py
@@ -167,7 +167,17 @@
     images = image_start.shape[0]
     steps_row = column_steps[None, :]
 
-    spread = lax.all_to_all(text_states, "text", split_axis=1, concat_axis=0, tiled=True)
+    n_image = lax.axis_size("image")
+    share = text_states.shape[1] // (n_text * n_image)
+    own = lax.dynamic_index_in_dim(
+        text_states.reshape(tok_dev, n_text, n_image, share),
+        lax.axis_index("image"),
+        2,
+        keepdims=False,
+    )
+    own = lax.all_to_all(own.transpose(1, 0, 2), "text", split_axis=0, concat_axis=0, tiled=True)
+    shares = lax.all_gather(own.reshape(n_text * tok_dev, share), "image", axis=0)
+    spread = shares.transpose(1, 0, 2).reshape(n_text * tok_dev, n_image * share)
     soft = 0.5 + 0.6 * jnp.tanh(0.5 * round_logits)
     weight_q = (steps_row * (grid_levels.astype(jnp.float32) + soft)).astype(jnp.bfloat16)
     weight_q = lax.optimization_barrier(weight_q)

time: 238 us -> 228 us (0.958)
  waiting for transfers between devices: 147 us -> 116 us
  blocking collectives: 0 us -> 20.7 us
  starting transfers between devices: 6.63 us -> 0.35 us
  local copies, waits for them, and re-layouts: 17.4 us -> 22.6 us
    all_to_all x1 -> x0, waiting for transfers between devices: 35.6 us -> none  [per_device(): lax.all_to_all(text_states, 'text', split_axis=1, concat_axis=0, tiled=True)]
    all_to_all x0 -> x1, blocking collectives: none -> 20.7 us  [per_device(): lax.all_to_all(own.transpose(1, 0, 2), 'text', split_axis=0, concat_axis=...]
    all_gather x0 -> x1, waiting for transfers between devices: none -> 9.03 us  [per_device(): lax.all_gather(own.reshape(n_text * tok_dev, share), 'image', axis=0)]
    all_to_all x1 -> x0, starting transfers between devices: 6.32 us -> none  [per_device(): lax.all_to_all(text_states, 'text', split_axis=1, concat_axis=0, tiled=True)]
    reduce_scatter x2, waiting for transfers between devices: 71.3 us -> 67.3 us  [per_device(): sums.append(lax.psum_scatter(part, 'text', scatter_dimension=0, tiled=True))]
    pad x2, local copies, waits for them, and re-layouts: 0.22 us -> 2.61 us  [window(): return jnp.pad(rows, ((0, KEYS_PAD - KEYS), (0, 0)))]
  transfers between devices with their start and end apart: 5 -> 5, of which waited for: 5 -> 5; matrix products, arithmetic and copies ran while one was open for 11% -> 12% of each run, Pallas kernels for 6% -> 7%
where the time goes in v3:
time: 228 us; the launch traced here: 227 us
  waiting for transfers between devices  116 us (51%)
  Pallas kernels  26.2 us (11%)
  local copies, waits for them, and re-layouts  22.6 us (10%)
  blocking collectives  20.7 us (9%)
  between operations  15.2 us (7%)
  other arithmetic  14.3 us (6%)
  matrix products  11.7 us (5%)
    reduce_scatter x2, waiting for transfers between devices, per_device(): sums.append(lax.psum_scatter(part, 'text', scatter_dimension=0, tiled=True))  67.3 us
    all_gather x2, waiting for transfers between devices, per_device(): grads.append(lax.all_gather(local, 'text', axis=0, tiled=True))  39.3 us
    pallas_call x2, Pallas kernels, final(): pl.pallas_call(final_kernel, out_shape=jax.ShapeDtypeStruct(logits.shape,...  21.6 us
    all_to_all x1, blocking collectives, per_device(): lax.all_to_all(own.transpose(1, 0, 2), 'text', split_axis=0, concat_axis=...  20.7 us
    unnamed x25, local copies, waits for them, and re-layouts  13.6 us
    convert_element_type x1, other arithmetic, per_device(): (steps_row * (grid_levels.astype(jnp.float32) + soft)).astype(jnp.bfloat16)  12.8 us
    dot_general x2, matrix products, per_device(): jnp.dot(spread, weight_q[:, c * width:(c + 1) * width], preferred_element...  11.7 us
    all_gather x1, waiting for transfers between devices, per_device(): lax.all_gather(own.reshape(n_text * tok_dev, share), 'image', axis=0)  9.03 us
  transfers between devices with their start and end apart: 5, of which 5 were waited for; matrix products, arithmetic and copies ran while one was open for 12% of the time, Pallas kernels for 7%

profile of v3, /device:TPU:0, one launch (start us, length us, event | category | flops | bytes accessed | tf_op | source)
XLA Modules:
  0.0 226.7 jit_solution(11279295691013222550)
XLA Ops:
  6.5 3.2 %copy.18 = bf16[128,8192]{0,1:T(8,128)(2,1)S(1)} copy(bf16[128,8192]{1,0:T(8,128)(2,1)} %param.9) | data formatting | bytes 4194304 | tf_op args[0]
  9.8 0.2 copy.19
  10.1 20.7 %all_to_all.5 = bf16[4,128,512]{2,1,0:T(8,128)(2,1)} all-to-all(bf16[4,128,512]{2,1,0:T(8,128)(2,1)S(1)} %bitcast.28), channel_id=1, replica_groups=mesh['groups'=2,'text'=4,'image'=4] {'text'}, dimensions={0} | all-to-all | bytes 1048576 | tf_op jit(solution)/shard_map/all_to_all | solution.py:178
  30.8 0.0 all-gather.4.cloned.1.call-update
  30.8 0.0 reduce-scatter.5.cloned.1.call-start
  30.9 12.8 %multiply_convert_fusion = bf16[2048,2048]{1,0:T(8,128)(2,1)} fusion(f32[2048,2048]{1,0:T(8,128)} %r_ref.3, bf16[2048,2048]{1,0:T(8,128)(2,1)} %param.10, f32[2048]{0:T(1024)S(1)} %copy-done.6), kind=kLoop, calls=%fused_computation | loop fusion | flops 29360128 | bytes 33562624 | tf_op jit(solution)/shard_map/convert_element_type | solution.py:182
  43.6 9.0 %all-gather.4.cloned.1.call-done = bf16[4,512,512]{2,1,0:T(8,128)(2,1)} async-done(((bf16[1,512,512]{2,1,0:T(8,128)(2,1)}), bf16[4,512,512]{2,1,0:T(8,128)(2,1)}) %all-gather.4.cloned.1.call-update) | async-done | bytes 2097168 | tf_op jit(solution)/shard_map/all_gather | solution.py:179
  52.6 2.8 %copy.20 = bf16[512,4,512]{0,2,1:T(8,128)(2,1)S(1)} copy(bf16[512,4,512]{2,0,1:T(8,128)(2,1)} %bitcast.26) | data formatting | bytes 4194304 | tf_op jit(solution)/shard_map/transpose | solution.py:180
  55.4 5.8 %fusion = f32[512,1024]{1,0:T(8,128)} fusion(bf16[512,2048]{0,1:T(8,128)(2,1)S(1)} %bitcast.19, bf16[2048,2048]{1,0:T(8,128)(2,1)} %multiply_convert_fusion), kind=kOutput, calls=%fused_computation.1 | convolution fusion | flops 2147483648 | bytes 8388608 | tf_op jit(solution)/shard_map/dot_general | solution.py:205
  61.3 0.0 reduce-scatter.5.cloned.1.call-update
  61.3 0.0 copy-start.11
  61.3 0.0 copy-start.10
  61.3 0.0 reduce-scatter.3.cloned.1.call-start
  61.4 5.9 %fusion.2 = f32[512,1024]{1,0:T(8,128)} fusion(bf16[512,2048]{0,1:T(8,128)(2,1)S(1)} %bitcast.20, bf16[2048,2048]{1,0:T(8,128)(2,1)} %multiply_convert_fusion), kind=kOutput, calls=%fused_computation.3 | convolution fusion | flops 2147483648 | bytes 8388608 | tf_op jit(solution)/shard_map/dot_general | solution.py:205
  67.2 0.0 reduce-scatter.3.cloned.1.call-update
  67.3 0.0 all-gather.8.cloned.1.call-start
  67.3 0.0 copy-done.11
  67.3 0.2 reduce-window.13
  67.5 0.1 convert_reduce_fusion
  67.6 0.2 select_reduce_fusion.1
  67.8 0.2 select_reduce_fusion
  68.0 0.2 reduce-window.14
  68.2 0.6 slice.10
  68.8 0.6 fusion.5
  70.8 2.7 %constant_dynamic-slice_fusion = (bf16[3202,256]{1,0:T(8,128)(2,1)S(1)}, bf16[3202,256]{1,0:T(8,128)(2,1)S(1)}) fusion(bf16[6404,256]{1,0:T(8,128)(2,1)} %param.14, s32[]{:T(128)S(6)} %select_n.24, bf16[6404,256]{1,0:T(8,128)(2,1)} %param.13), kind=kLoop, calls=%fused_computation.14 | loop fusion | bytes 6557700 | tf_op jit(solution)/shard_map/dynamic_slice | solution.py:195
  73.5 0.0 copy-start.7
  73.5 1.3 pad.8.v_ref
  74.8 1.3 pad.7.k_ref
  76.7 0.1 pad_add_fusion.bounds_ref
  76.8 28.6 %reduce-scatter.5.cloned.1.call-done.q_ref = f32[128,1024]{1,0:T(8,128)} async-done(((f32[512,1024]{1,0:T(8,128)}), f32[128,1024]{1,0:T(8,128)}) %reduce-scatter.5.cloned.1.call-update) | async-done | bytes 524304 | tf_op jit(solution)/shard_map/reduce_scatter | solution.py:208
  105.4 1.5 copy-done
  106.8 1.5 copy-done.2
  108.3 1.0 copy-done.9
  109.3 2.3 %attention.3 = bf16[128,1024]{1,0:T(8,128)(2,1)} custom-call(s32[2]{0:T(128)S(1)} %pad_add_fusion.bounds_ref, f32[128,1024]{1,0:T(8,128)S(1)} %copy-done.9, bf16[3328,256]{1,0:T(8,128)(2,1)S(1)} %copy-done.2, bf16[3328,256]{1,0:T(8,128)(2,1)S(1)} %copy-done, bf16[128,2048]{1,0:T(8,128)(2,1)S(1)} %copy-done.7), custom_call_target="tpu_custom_call" | custom-call | flops 4362076160 | bytes 2752512 | tf_op jit(solution)/shard_map/attention/pallas_call | solution.py:87
  111.6 0.0 all-gather.8.cloned.1.call-update
  111.6 0.2 all-gather.6.cloned.1.call-start
  111.9 38.7 %reduce-scatter.3.cloned.1.call-done.q_ref = f32[128,1024]{1,0:T(8,128)} async-done(((f32[512,1024]{1,0:T(8,128)}), f32[128,1024]{1,0:T(8,128)}) %reduce-scatter.3.cloned.1.call-update) | async-done | bytes 524304 | tf_op jit(solution)/shard_map/reduce_scatter | solution.py:208
  150.6 1.5 copy-done.1
  152.0 1.5 copy-done.3
  153.5 1.0 copy-done.8
  154.5 2.3 %attention.2 = bf16[128,1024]{1,0:T(8,128)(2,1)} custom-call(s32[2]{0:T(128)S(1)} %pad_add_fusion.bounds_ref, f32[128,1024]{1,0:T(8,128)S(1)} %copy-done.8, bf16[3328,256]{1,0:T(8,128)(2,1)S(1)} %copy-done.3, bf16[3328,256]{1,0:T(8,128)(2,1)S(1)} %copy-done.1, bf16[128,2048]{1,0:T(8,128)(2,1)S(1)} %copy-done.7), custom_call_target="tpu_custom_call" | custom-call | flops 4362076160 | bytes 2752512 | tf_op jit(solution)/shard_map/attention/pallas_call | solution.py:87
  156.9 0.0 all-gather.6.cloned.1.call-update
  156.9 22.4 %all-gather.8.cloned.1.call-done.g_ref = bf16[512,1024]{1,0:T(8,128)(2,1)} async-done(((bf16[128,1024]{1,0:T(8,128)(2,1)}), bf16[512,1024]{1,0:T(8,128)(2,1)}) %all-gather.8.cloned.1.call-update) | async-done | bytes 1048592 | tf_op jit(solution)/shard_map/all_gather | solution.py:211
  179.3 1.2 copy-done.4
  180.5 10.8 %final.2.rest_0_ = f32[2048,2048]{1,0:T(8,128)} custom-call(bf16[2048,512]{1,0:T(8,128)(2,1)S(1)} %bitcast.21, bf16[512,1024]{1,0:T(8,128)(2,1)S(1)} %copy-done.4, f32[2048,2048]{1,0:T(8,128)} %r_ref.3, f32[1,2048]{1,0:T(1,128)S(1)} %bitcast.23), custom_call_target="tpu_custom_call" | custom-call | flops 2147483648 | bytes 19922944 | tf_op jit(solution)/shard_map/final/pallas_call | solution.py:135
  191.3 16.8 %all-gather.6.cloned.1.call-done.g_ref = bf16[512,1024]{1,0:T(8,128)(2,1)} async-done(((bf16[128,1024]{1,0:T(8,128)(2,1)}), bf16[512,1024]{1,0:T(8,128)(2,1)}) %all-gather.6.cloned.1.call-update) | async-done | bytes 1048592 | tf_op jit(solution)/shard_map/all_gather | solution.py:211
  208.2 1.2 copy-done.5
  209.4 10.8 %final.3 = f32[2048,2048]{1,0:T(8,128)} custom-call(bf16[2048,512]{1,0:T(8,128)(2,1)S(1)} %bitcast.22, bf16[512,1024]{1,0:T(8,128)(2,1)S(1)} %copy-done.5, f32[2048,2048]{1,0:T(8,128)} %r_ref.3, f32[1,2048]{1,0:T(1,128)S(1)} %bitcast.24, f32[2048,2048]{1,0:T(8,128)} %final.2.rest_0_), custom_call_target="tpu_custom_call", output_to_operand_aliasing={{}: (4, {})} | custom-call | flops 2147483648 | bytes 19922944 | tf_op jit(solution)/shard_map/final/pallas_call | solution.py:135
  (15 shorter events, 0.1 us)
Async XLA Ops:
  6.5 24.3 %copy-start.6 = (f32[2048]{0:T(1024)S(1)}, f32[2048]{0:T(1024)}, u32[]{:S(2)}) copy-start(f32[2048]{0:T(1024)} %param.12) | copy-start | bytes 24580
  6.5 46.1 %all-gather.4.cloned.1.call-start = ((), (), s32[]{:S(2)}) async-start(), calls=%async_computation.3 | async-start | bytes 2621440 | tf_op jit(solution)/shard_map/all_gather | solution.py:179
  30.8 74.5 %reduce-scatter.5.cloned.1.call-start = ((), (), s32[]{:S(2)}) async-start(), calls=%async_computation.6 | async-start | bytes 2621440 | tf_op jit(solution)/shard_map/reduce_scatter | solution.py:208
  61.3 6.0 %copy-start.11 = (s32[3]{0:T(128)S(1)}, s32[3]{0:T(128)}, u32[]{:S(2)}) copy-start(s32[3]{0:T(128)} %param.16) | copy-start | bytes 40
  61.3 6.5 %copy-start.10 = (s32[4]{0:T(128)S(1)}, s32[4]{0:T(128)}, u32[]{:S(2)}) copy-start(s32[4]{0:T(128)} %param.17) | copy-start | bytes 52
  61.3 89.3 %reduce-scatter.3.cloned.1.call-start = ((), (), s32[]{:S(2)}) async-start(), calls=%async_computation.4 | async-start | bytes 2621440 | tf_op jit(solution)/shard_map/reduce_scatter | solution.py:208
  67.3 112.0 %all-gather.8.cloned.1.call-start = ((), (), s32[]{:S(2)}) async-start(), calls=%async_computation.7 | async-start | bytes 1310720 | tf_op jit(solution)/shard_map/all_gather | solution.py:211
  73.5 31.9 %copy-start.7 = (bf16[128,2048]{1,0:T(8,128)(2,1)S(1)}, bf16[128,2048]{1,0:T(8,128)(2,1)}, u32[]{:S(2)}) copy-start(bf16[128,2048]{1,0:T(8,128)(2,1)} %t_ref.3) | copy-start | bytes 1572868
  105.3 1.5 copy-start
  106.8 1.5 copy-start.2
  108.3 1.0 copy-start.9
  111.6 96.5 %all-gather.6.cloned.1.call-start = ((), (), s32[]{:S(2)}) async-start(), calls=%async_computation.5 | async-start | bytes 1310720 | tf_op jit(solution)/shard_map/all_gather | solution.py:211
  150.6 1.5 copy-start.1
  152.0 1.5 copy-start.3
  153.5 1.0 copy-start.8
  179.3 1.2 copy-start.4
  208.2 1.2 copy-start.5
Sparse Core Ops, SparseCore 0:
  30.9 21.6 all-gather.3
  61.4 43.8 reduce-scatter.4
  107.7 42.7 reduce-scatter.2
  152.0 27.2 all-gather.7
  180.7 27.4 all-gather.5

commit v4 on v3

--- a/solution.py
+++ b/solution.py
@@ -149,6 +149,31 @@
     )(*args)
 
 
+FIXED = 32767.0
+
+
+def exchange_sum(part, tok_dev):
+    n_text = lax.axis_size("text")
+    me = lax.axis_index("text")
+    width = part.shape[1]
+    heads = width // HD
+
+    def rows_of(owner):
+        return lax.dynamic_slice_in_dim(part, owner * tok_dev, tok_dev, 0)
+
+    total = rows_of(me).reshape(tok_dev, heads, HD)
+    for shift in range(1, n_text):
+        perm = [(i, (i + shift) % n_text) for i in range(n_text)]
+        rows = rows_of((me + shift) % n_text).reshape(tok_dev, heads, HD)
+        largest = jnp.maximum(jnp.max(jnp.abs(rows), axis=-1), 1e-30)
+        levels = jnp.round(rows * (FIXED / largest)[..., None]).astype(jnp.int16)
+        levels = lax.ppermute(levels.reshape(tok_dev, width), "text", perm)
+        largest = lax.ppermute(largest.T, "text", perm).T
+        levels = levels.reshape(tok_dev, heads, HD).astype(jnp.float32)
+        total = total + levels * (largest * (1.0 / FIXED))[..., None]
+    return total.reshape(tok_dev, width)
+
+
 def per_device(
     text_states,
     grid_levels,
@@ -205,7 +230,7 @@
         part = jnp.dot(
             spread, weight_q[:, c * width : (c + 1) * width], preferred_element_type=jnp.float32
         )
-        sums.append(lax.psum_scatter(part, "text", scatter_dimension=0, tiled=True))
+        sums.append(exchange_sum(part, tok_dev))
     for c in range(CHUNKS):
         local = attention(bounds, sums[c], keys, values, target_out, c)
         grads.append(lax.all_gather(local, "text", axis=0, tiled=True))

time: 228 us -> 234 us (1.026)
  waiting for transfers between devices: 116 us -> 64.1 us
  starting transfers between devices: 0.35 us -> 41.7 us
  other arithmetic: 14.3 us -> 33.5 us
  matrix products: 11.7 us -> 8.41 us
    reduce_scatter x2 -> x0, waiting for transfers between devices: 67.3 us -> none  [per_device(): sums.append(lax.psum_scatter(part, 'text', scatter_dimension=0, tiled=True))]
    ppermute x0 -> x12, starting transfers between devices: none -> 41.6 us  [the longest x6 22 us: exchange_sum(): levels = lax.ppermute(levels.reshape(tok_dev, width), 'text', perm)]
    ppermute x0 -> x12, waiting for transfers between devices: none -> 28.9 us  [the longest x6 28.9 us: exchange_sum(): levels = lax.ppermute(levels.reshape(tok_dev, width), 'text', perm)]
    all_gather x1, waiting for transfers between devices: 9.03 us -> 0.01 us  [per_device(): lax.all_gather(own.reshape(n_text * tok_dev, share), 'image', axis=0)]
    reduce_max x0 -> x6, other arithmetic: none -> 5.4 us  [exchange_sum(): largest = jnp.maximum(jnp.max(jnp.abs(rows), axis=-1), 1e-30)]
    all_gather x2, waiting for transfers between devices: 39.3 us -> 35.2 us  [per_device(): grads.append(lax.all_gather(local, 'text', axis=0, tiled=True))]
    convert_element_type x0 -> x2, other arithmetic: none -> 3.85 us  [exchange_sum(): levels = jnp.round(rows * (FIXED / largest)[..., None]).astype(jnp.int16)]
    dot_general x2, matrix products: 11.7 us -> 8.41 us  [per_device(): jnp.dot(spread, weight_q[:, c * width:(c + 1) * width], preferred_element...]
  transfers between devices with their start and end apart: 5 -> 15, of which waited for: 5 -> 5; matrix products, arithmetic and copies ran while one was open for 12% -> 19% of each run, Pallas kernels for 7% -> 7%
where the time goes in v4:
time: 234 us; the launch traced here: 232 us
  waiting for transfers between devices  64.1 us (27%)
  starting transfers between devices  41.7 us (18%)
  other arithmetic  33.5 us (14%)
  Pallas kernels  26.1 us (11%)
  local copies, waits for them, and re-layouts  22.3 us (10%)
  blocking collectives  20.7 us (9%)
  between operations  15.4 us (7%)
  matrix products  8.41 us (4%)
    all_gather x2, waiting for transfers between devices, per_device(): grads.append(lax.all_gather(local, 'text', axis=0, tiled=True))  35.2 us
    ppermute x6, waiting for transfers between devices, exchange_sum(): levels = lax.ppermute(levels.reshape(tok_dev, width), 'text', perm)  28.9 us
    ppermute x6, starting transfers between devices, exchange_sum(): levels = lax.ppermute(levels.reshape(tok_dev, width), 'text', perm)  22 us
    pallas_call x2, Pallas kernels, final(): pl.pallas_call(final_kernel, out_shape=jax.ShapeDtypeStruct(logits.shape,...  21.5 us
    all_to_all x1, blocking collectives, per_device(): lax.all_to_all(own.transpose(1, 0, 2), 'text', split_axis=0, concat_axis=...  20.7 us
    ppermute x6, starting transfers between devices, exchange_sum(): largest = lax.ppermute(largest.T, 'text', perm).T  19.7 us
    convert_element_type x1, other arithmetic, per_device(): (steps_row * (grid_levels.astype(jnp.float32) + soft)).astype(jnp.bfloat16)  12.7 us
    unnamed x35, local copies, waits for them, and re-layouts  10.8 us
  transfers between devices with their start and end apart: 15, of which 5 were waited for; matrix products, arithmetic and copies ran while one was open for 19% of the time, Pallas kernels for 7%

profile of v4, /device:TPU:0, one launch (start us, length us, event | category | flops | bytes accessed | tf_op | source)
XLA Modules:
  0.0 232.4 jit_solution(7985636498867105157)
XLA Ops:
  6.5 3.2 %copy.18 = bf16[128,8192]{0,1:T(8,128)(2,1)S(1)} copy(bf16[128,8192]{1,0:T(8,128)(2,1)} %param.9) | data formatting | bytes 4194304 | tf_op args[0]
  10.1 20.7 %all_to_all.5 = bf16[4,128,512]{2,1,0:T(8,128)(2,1)} all-to-all(bf16[4,128,512]{2,1,0:T(8,128)(2,1)S(1)} %bitcast.157), channel_id=1, replica_groups=mesh['groups'=2,'text'=4,'image'=4] {'text'}, dimensions={0} | all-to-all | bytes 1048576 | tf_op jit(solution)/shard_map/all_to_all | solution.py:203
  34.3 2.8 %constant_dynamic-slice_fusion = (bf16[3202,256]{1,0:T(8,128)(2,1)S(1)}, bf16[3202,256]{1,0:T(8,128)(2,1)S(1)}) fusion(bf16[6404,256]{1,0:T(8,128)(2,1)} %param.14, s32[]{:T(128)S(6)} %select_n.68, bf16[6404,256]{1,0:T(8,128)(2,1)} %param.13), kind=kLoop, calls=%fused_computation.59 | loop fusion | bytes 6557700 | tf_op jit(solution)/shard_map/dynamic_slice | solution.py:220
  37.1 1.3 pad.8.v_ref
  38.5 1.3 pad.7.k_ref
  39.8 12.7 %multiply_convert_fusion = bf16[2048,2048]{1,0:T(8,128)(2,1)} fusion(f32[2048,2048]{1,0:T(8,128)} %r_ref.3, bf16[2048,2048]{1,0:T(8,128)(2,1)} %param.10, f32[2048]{0:T(1024)S(1)} %copy-done.6), kind=kLoop, calls=%fused_computation | loop fusion | flops 29360128 | bytes 33562624 | tf_op jit(solution)/shard_map/convert_element_type | solution.py:207
  53.1 2.8 %copy.20 = bf16[512,4,512]{0,2,1:T(8,128)(2,1)S(1)} copy(bf16[512,4,512]{2,0,1:T(8,128)(2,1)} %bitcast.154) | data formatting | bytes 4194304 | tf_op jit(solution)/shard_map/transpose | solution.py:205
  55.9 6.0 %fusion = f32[512,1024]{1,0:T(8,128)} fusion(bf16[512,2048]{0,1:T(8,128)(2,1)S(1)} %bitcast.141, bf16[2048,2048]{1,0:T(8,128)(2,1)} %multiply_convert_fusion), kind=kOutput, calls=%fused_computation.1 | convolution fusion | flops 2147483648 | bytes 8388608 | tf_op jit(solution)/shard_map/dot_general | solution.py:230
  62.0 2.4 %fusion.2 = f32[512,1024]{1,0:T(8,128)S(1)} fusion(bf16[512,2048]{0,1:T(8,128)(2,1)S(1)} %bitcast.142, bf16[2048,2048]{1,0:T(8,128)(2,1)S(1)} %copy-done.8), kind=kOutput, calls=%fused_computation.3 | convolution fusion | flops 2147483648 | bytes 8388608 | tf_op jit(solution)/shard_map/dot_general | solution.py:230
  64.4 1.3 copy-done.9
  65.9 0.9 copy.21
  66.8 1.2 reduce_max.54
  68.1 1.1 collective-permute-start.1
  69.2 0.9 copy.27
  70.1 1.2 reduce_max.56
  72.9 1.5 abs_bitcast_fusion.2
  74.4 0.9 copy.30
  75.3 1.2 reduce_max.57
  77.2 1.5 collective-permute-start.7
  78.7 0.9 copy.36
  79.6 1.2 reduce_max.59
  80.8 0.6 maximum_divide_fusion
  81.5 2.3 %collective-permute-start.11 = (f32[8,128]{0,1:T(8,128)}, f32[8,128]{0,1:T(8,128)}, u32[]{:S(2)}, u32[]{:S(2)}) collective-permute-start(f32[8,128]{0,1:T(8,128)} %get-tuple-element.22), channel_id=1, source_target_pairs={{0,12},{4,0},{8,4},{12,8},{1,13},{5,1},{9,5},{13,9},{2,14},{6,2},{... | collective-permute-start | bytes 12296 | tf_op jit(solution)/shard_map/ppermute | solution.py:171
  84.2 0.7 collective-permute-start.9
  85.5 1.9 fusion.12
  87.4 1.0 collective-permute-start.6
  88.4 1.5 collective-permute-start.8
  89.9 0.8 multiply_bitcast_fusion.2
  90.7 2.9 %collective-permute-start.10 = (s16[128,1024]{1,0:T(8,128)(2,1)S(1)}, s16[128,1024]{1,0:T(8,128)(2,1)S(1)}, u32[]{:S(2)}, u32[]{:S(2)}) collective-permute-start(s16[128,1024]{1,0:T(8,128)(2,1)S(1)} %get-tuple-element.7), channel_id=1, source_target_pairs={{0,12},{4,0},{8,4},{12,8},{1,13},{5,1},{9,5},{13,9},{2,14},{6,2},{... | collective-permute-start | bytes 786440 | tf_op jit(solution)/shard_map/ppermute | solution.py:170
  93.6 0.8 multiply_bitcast_fusion
  94.8 3.8 %collective-permute-done.6 = s16[128,1024]{1,0:T(8,128)(2,1)S(1)} collective-permute-done((s16[128,1024]{1,0:T(8,128)(2,1)S(1)}, s16[128,1024]{1,0:T(8,128)(2,1)S(1)}, u32[]{:S(2)}, u32[]{:S(2)}) %collective-permute-start.6) | collective-permute-done | bytes 262176 | tf_op jit(solution)/shard_map/ppermute | solution.py:170
  98.6 13.8 %collective-permute-start.3 = (f32[8,128]{0,1:T(8,128)S(1)}, f32[8,128]{0,1:T(8,128)S(1)}, u32[]{:S(2)}, u32[]{:S(2)}) collective-permute-start(f32[8,128]{0,1:T(8,128)S(1)} %copy-done.11), channel_id=1, source_target_pairs={{0,8},{4,12},{8,0},{12,4},{1,9},{5,13},{9,1},{13,5},{2,10},{6,14},... | collective-permute-start | bytes 12296 | tf_op jit(solution)/shard_map/ppermute | solution.py:171
  113.0 1.6 fusion.4.q_ref
  114.6 2.3 attention.3
  117.6 1.9 fusion.21
  119.5 13.3 %collective-permute-start = (s16[128,1024]{1,0:T(8,128)(2,1)S(1)}, s16[128,1024]{1,0:T(8,128)(2,1)S(1)}, u32[]{:S(2)}, u32[]{:S(2)}) collective-permute-start(s16[128,1024]{1,0:T(8,128)(2,1)S(1)} %get-tuple-element.11), channel_id=1, source_target_pairs={{0,4},{4,8},{8,12},{12,0},{1,5},{5,9},{9,13},{13,1},{2,6},{6,10},{... | collective-permute-start | bytes 786440 | tf_op jit(solution)/shard_map/ppermute | solution.py:170
  132.9 3.3 %collective-permute-start.2 = (s16[128,1024]{1,0:T(8,128)(2,1)S(1)}, s16[128,1024]{1,0:T(8,128)(2,1)S(1)}, u32[]{:S(2)}, u32[]{:S(2)}) collective-permute-start(s16[128,1024]{1,0:T(8,128)(2,1)S(1)} %get-tuple-element.12), channel_id=1, source_target_pairs={{0,8},{4,12},{8,0},{12,4},{1,9},{5,13},{9,1},{13,5},{2,10},{6,14},... | collective-permute-start | bytes 786440 | tf_op jit(solution)/shard_map/ppermute | solution.py:170
  136.2 0.9 multiply_bitcast_fusion.5
  137.1 6.7 %collective-permute-done = s16[128,1024]{1,0:T(8,128)(2,1)S(1)} collective-permute-done((s16[128,1024]{1,0:T(8,128)(2,1)S(1)}, s16[128,1024]{1,0:T(8,128)(2,1)S(1)}, u32[]{:S(2)}, u32[]{:S(2)}) %collective-permute-start) | collective-permute-done | bytes 262176 | tf_op jit(solution)/shard_map/ppermute | solution.py:170
  143.7 18.4 %collective-permute-done.2 = s16[128,1024]{1,0:T(8,128)(2,1)S(1)} collective-permute-done((s16[128,1024]{1,0:T(8,128)(2,1)S(1)}, s16[128,1024]{1,0:T(8,128)(2,1)S(1)}, u32[]{:S(2)}, u32[]{:S(2)}) %collective-permute-start.2) | collective-permute-done | bytes 262176 | tf_op jit(solution)/shard_map/ppermute | solution.py:170
  162.7 1.6 fusion.13.q_ref
  164.3 2.3 attention.2
  166.7 3.5 %all-gather.8.cloned.1.call-done.g_ref = bf16[512,1024]{1,0:T(8,128)(2,1)} async-done(((bf16[128,1024]{1,0:T(8,128)(2,1)}), bf16[512,1024]{1,0:T(8,128)(2,1)}) %all-gather.8.cloned.1.call-update) | async-done | bytes 1048592 | tf_op jit(solution)/shard_map/all_gather | solution.py:236
  170.2 1.2 copy-done.4
  171.4 10.8 %final.2.rest_0_ = f32[2048,2048]{1,0:T(8,128)} custom-call(bf16[2048,512]{1,0:T(8,128)(2,1)S(1)} %bitcast.143, bf16[512,1024]{1,0:T(8,128)(2,1)S(1)} %copy-done.4, f32[2048,2048]{1,0:T(8,128)} %r_ref.3, f32[1,2048]{1,0:T(1,128)S(1)} %bitcast.145), custom_call_target="tpu_custom_call" | custom-call | flops 2147483648 | bytes 19922944 | tf_op jit(solution)/shard_map/final/pallas_call | solution.py:135
  182.1 31.7 %all-gather.6.cloned.1.call-done.g_ref = bf16[512,1024]{1,0:T(8,128)(2,1)} async-done(((bf16[128,1024]{1,0:T(8,128)(2,1)}), bf16[512,1024]{1,0:T(8,128)(2,1)}) %all-gather.6.cloned.1.call-update) | async-done | bytes 1048592 | tf_op jit(solution)/shard_map/all_gather | solution.py:236
  213.9 1.2 copy-done.5
  215.1 10.8 %final.3 = f32[2048,2048]{1,0:T(8,128)} custom-call(bf16[2048,512]{1,0:T(8,128)(2,1)S(1)} %bitcast.144, bf16[512,1024]{1,0:T(8,128)(2,1)S(1)} %copy-done.5, f32[2048,2048]{1,0:T(8,128)} %r_ref.3, f32[1,2048]{1,0:T(1,128)S(1)} %bitcast.146, f32[2048,2048]{1,0:T(8,128)} %final.2.rest_0_), custom_call_target="tpu_custom_call", output_to_operand_aliasing={{}: (4, {})} | custom-call | flops 2147483648 | bytes 19922944 | tf_op jit(solution)/shard_map/final/pallas_call | solution.py:135
  (79 shorter events, 8.1 us)
Async XLA Ops:
  6.5 46.6 %all-gather.4.cloned.1.call-start = ((), (), s32[]{:S(2)}) async-start(), calls=%async_computation.1 | async-start | bytes 2621440 | tf_op jit(solution)/shard_map/all_gather | solution.py:204
  6.5 24.4 %copy-start.13 = (s32[3]{0:T(128)S(1)}, s32[3]{0:T(128)}, u32[]{:S(2)}) copy-start(s32[3]{0:T(128)} %param.16) | copy-start | bytes 40
  6.5 24.9 %copy-start.12 = (s32[4]{0:T(128)S(1)}, s32[4]{0:T(128)}, u32[]{:S(2)}) copy-start(s32[4]{0:T(128)} %param.17) | copy-start | bytes 52
  30.8 139.3 %all-gather.8.cloned.1.call-start = ((), (), s32[]{:S(2)}) async-start(), calls=%async_computation.3 | async-start | bytes 1310720 | tf_op jit(solution)/shard_map/all_gather | solution.py:236
  37.1 2.7 %copy-start.6 = (f32[2048]{0:T(1024)S(1)}, f32[2048]{0:T(1024)}, u32[]{:S(2)}) copy-start(f32[2048]{0:T(1024)} %param.12) | copy-start | bytes 24580
  55.9 6.0 %copy-start.8 = (bf16[2048,2048]{1,0:T(8,128)(2,1)S(1)}, bf16[2048,2048]{1,0:T(8,128)(2,1)}, u32[]{:S(2)}) copy-start(bf16[2048,2048]{1,0:T(8,128)(2,1)} %multiply_convert_fusion) | copy-start | bytes 25165828
  64.3 1.3 copy-start.9
  68.1 68.1 %collective-permute-start.1 = (f32[8,128]{0,1:T(8,128)S(1)}, f32[8,128]{0,1:T(8,128)}, u32[]{:S(2)}, u32[]{:S(2)}) collective-permute-start(f32[8,128]{0,1:T(8,128)S(1)} %get-tuple-element.24), channel_id=1, source_target_pairs={{0,4},{4,8},{8,12},{12,0},{1,5},{5,9},{9,13},{13,1},{2,6},{6,10},{... | collective-permute-start | bytes 12296 | tf_op jit(solution)/shard_map/ppermute | solution.py:171
  77.2 11.2 %collective-permute-start.7 = (f32[8,128]{0,1:T(8,128)}, f32[8,128]{0,1:T(8,128)}, u32[]{:S(2)}, u32[]{:S(2)}) collective-permute-start(f32[8,128]{0,1:T(8,128)} %get-tuple-element.18), channel_id=1, source_target_pairs={{0,4},{4,8},{8,12},{12,0},{1,5},{5,9},{9,13},{13,1},{2,6},{6,10},{... | collective-permute-start | bytes 12296 | tf_op jit(solution)/shard_map/ppermute | solution.py:171
  81.5 9.2 %collective-permute-start.11 = (f32[8,128]{0,1:T(8,128)}, f32[8,128]{0,1:T(8,128)}, u32[]{:S(2)}, u32[]{:S(2)}) collective-permute-start(f32[8,128]{0,1:T(8,128)} %get-tuple-element.22), channel_id=1, source_target_pairs={{0,12},{4,0},{8,4},{12,8},{1,13},{5,1},{9,5},{13,9},{2,14},{6,2},{... | collective-permute-start | bytes 12296 | tf_op jit(solution)/shard_map/ppermute | solution.py:171
  84.1 10.3 %copy-start.10 = (f32[8,128]{0,1:T(8,128)S(1)}, f32[8,128]{0,1:T(8,128)}, u32[]{:S(2)}) copy-start(f32[8,128]{0,1:T(8,128)} %get-tuple-element.28) | copy-start | bytes 12292
  84.1 14.5 %copy-start.11 = (f32[8,128]{0,1:T(8,128)S(1)}, f32[8,128]{0,1:T(8,128)}, u32[]{:S(2)}) copy-start(f32[8,128]{0,1:T(8,128)} %get-tuple-element.26) | copy-start | bytes 12292
  84.2 10.3 %collective-permute-start.9 = (f32[8,128]{0,1:T(8,128)S(1)}, f32[8,128]{0,1:T(8,128)S(1)}, u32[]{:S(2)}, u32[]{:S(2)}) collective-permute-start(f32[8,128]{0,1:T(8,128)S(1)} %get-tuple-element.20), channel_id=1, source_target_pairs={{0,8},{4,12},{8,0},{12,4},{1,9},{5,13},{9,1},{13,5},{2,10},{6,14},... | collective-permute-start | bytes 12296 | tf_op jit(solution)/shard_map/ppermute | solution.py:171
  87.4 27.2 %copy-start = (bf16[3328,256]{1,0:T(8,128)(2,1)S(1)}, bf16[3328,256]{1,0:T(8,128)(2,1)}, u32[]{:S(2)}) copy-start(bf16[3328,256]{1,0:T(8,128)(2,1)} %pad.8.v_ref) | copy-start | bytes 5111812
  87.4 27.2 %copy-start.2 = (bf16[3328,256]{1,0:T(8,128)(2,1)S(1)}, bf16[3328,256]{1,0:T(8,128)(2,1)}, u32[]{:S(2)}) copy-start(bf16[3328,256]{1,0:T(8,128)(2,1)} %pad.7.k_ref) | copy-start | bytes 5111812
  87.4 27.2 %copy-start.7 = (bf16[128,2048]{1,0:T(8,128)(2,1)S(1)}, bf16[128,2048]{1,0:T(8,128)(2,1)}, u32[]{:S(2)}) copy-start(bf16[128,2048]{1,0:T(8,128)(2,1)} %t_ref.3) | copy-start | bytes 1572868
  87.4 11.2 %collective-permute-start.6 = (s16[128,1024]{1,0:T(8,128)(2,1)S(1)}, s16[128,1024]{1,0:T(8,128)(2,1)S(1)}, u32[]{:S(2)}, u32[]{:S(2)}) collective-permute-start(s16[128,1024]{1,0:T(8,128)(2,1)S(1)} %get-tuple-element.5), channel_id=1, source_target_pairs={{0,4},{4,8},{8,12},{12,0},{1,5},{5,9},{9,13},{13,1},{2,6},{6,10},{... | collective-permute-start | bytes 786440 | tf_op jit(solution)/shard_map/ppermute | solution.py:170
  88.4 24.0 %collective-permute-start.8 = (s16[128,1024]{1,0:T(8,128)(2,1)S(1)}, s16[128,1024]{1,0:T(8,128)(2,1)S(1)}, u32[]{:S(2)}, u32[]{:S(2)}) collective-permute-start(s16[128,1024]{1,0:T(8,128)(2,1)S(1)} %get-tuple-element.6), channel_id=1, source_target_pairs={{0,8},{4,12},{8,0},{12,4},{1,9},{5,13},{9,1},{13,5},{2,10},{6,14},... | collective-permute-start | bytes 786440 | tf_op jit(solution)/shard_map/ppermute | solution.py:170
  90.7 21.7 %collective-permute-start.10 = (s16[128,1024]{1,0:T(8,128)(2,1)S(1)}, s16[128,1024]{1,0:T(8,128)(2,1)S(1)}, u32[]{:S(2)}, u32[]{:S(2)}) collective-permute-start(s16[128,1024]{1,0:T(8,128)(2,1)S(1)} %get-tuple-element.7), channel_id=1, source_target_pairs={{0,12},{4,0},{8,4},{12,8},{1,13},{5,1},{9,5},{13,9},{2,14},{6,2},{... | collective-permute-start | bytes 786440 | tf_op jit(solution)/shard_map/ppermute | solution.py:170
  94.5 42.5 %collective-permute-start.5 = (f32[8,128]{0,1:T(8,128)S(1)}, f32[8,128]{0,1:T(8,128)S(1)}, u32[]{:S(2)}, u32[]{:S(2)}) collective-permute-start(f32[8,128]{0,1:T(8,128)S(1)} %copy-done.10), channel_id=1, source_target_pairs={{0,12},{4,0},{8,4},{12,8},{1,13},{5,1},{9,5},{13,9},{2,14},{6,2},{... | collective-permute-start | bytes 12296 | tf_op jit(solution)/shard_map/ppermute | solution.py:171
  98.6 38.4 %collective-permute-start.3 = (f32[8,128]{0,1:T(8,128)S(1)}, f32[8,128]{0,1:T(8,128)S(1)}, u32[]{:S(2)}, u32[]{:S(2)}) collective-permute-start(f32[8,128]{0,1:T(8,128)S(1)} %copy-done.11), channel_id=1, source_target_pairs={{0,8},{4,12},{8,0},{12,4},{1,9},{5,13},{9,1},{13,5},{2,10},{6,14},... | collective-permute-start | bytes 12296 | tf_op jit(solution)/shard_map/ppermute | solution.py:171
  117.0 96.9 %all-gather.6.cloned.1.call-start = ((), (), s32[]{:S(2)}) async-start(), calls=%async_computation.2 | async-start | bytes 1310720 | tf_op jit(solution)/shard_map/all_gather | solution.py:236
  119.5 44.8 %copy-start.1 = (bf16[3328,256]{1,0:T(8,128)(2,1)S(1)}, bf16[3328,256]{1,0:T(8,128)(2,1)}, u32[]{:S(2)}) copy-start(bf16[3328,256]{1,0:T(8,128)(2,1)} %pad.8.v_ref) | copy-start | bytes 5111812
  119.5 44.8 %copy-start.3 = (bf16[3328,256]{1,0:T(8,128)(2,1)S(1)}, bf16[3328,256]{1,0:T(8,128)(2,1)}, u32[]{:S(2)}) copy-start(bf16[3328,256]{1,0:T(8,128)(2,1)} %pad.7.k_ref) | copy-start | bytes 5111812
  119.5 24.2 %collective-permute-start = (s16[128,1024]{1,0:T(8,128)(2,1)S(1)}, s16[128,1024]{1,0:T(8,128)(2,1)S(1)}, u32[]{:S(2)}, u32[]{:S(2)}) collective-permute-start(s16[128,1024]{1,0:T(8,128)(2,1)S(1)} %get-tuple-element.11), channel_id=1, source_target_pairs={{0,4},{4,8},{8,12},{12,0},{1,5},{5,9},{9,13},{13,1},{2,6},{6,10},{... | collective-permute-start | bytes 786440 | tf_op jit(solution)/shard_map/ppermute | solution.py:170
  132.9 29.2 %collective-permute-start.2 = (s16[128,1024]{1,0:T(8,128)(2,1)S(1)}, s16[128,1024]{1,0:T(8,128)(2,1)S(1)}, u32[]{:S(2)}, u32[]{:S(2)}) collective-permute-start(s16[128,1024]{1,0:T(8,128)(2,1)S(1)} %get-tuple-element.12), channel_id=1, source_target_pairs={{0,8},{4,12},{8,0},{12,4},{1,9},{5,13},{9,1},{13,5},{2,10},{6,14},... | collective-permute-start | bytes 786440 | tf_op jit(solution)/shard_map/ppermute | solution.py:170
  136.2 25.9 %collective-permute-start.4 = (s16[128,1024]{1,0:T(8,128)(2,1)S(1)}, s16[128,1024]{1,0:T(8,128)(2,1)S(1)}, u32[]{:S(2)}, u32[]{:S(2)}) collective-permute-start(s16[128,1024]{1,0:T(8,128)(2,1)S(1)} %get-tuple-element.13), channel_id=1, source_target_pairs={{0,12},{4,0},{8,4},{12,8},{1,13},{5,1},{9,5},{13,9},{2,14},{6,2},{... | collective-permute-start | bytes 786440 | tf_op jit(solution)/shard_map/ppermute | solution.py:170
  170.2 1.2 copy-start.4
  213.9 1.2 copy-start.5
Sparse Core Ops, SparseCore 0:
  30.9 21.7 all-gather.3
  117.1 53.0 all-gather.7
  171.7 42.0 all-gather.5

commit v5 on v3

--- a/solution.py
+++ b/solution.py
@@ -15,7 +15,7 @@
 MAX_SEEN = 2
 KEYS = MAX_SEEN * IMG_TOK
 KEYS_PAD = -(-KEYS // 256) * 256
-CHUNKS = 2
+CHUNKS = 4
 NEG = -1e30
 
 

time: 228 us -> 261 us (1.14)
  blocking collectives: 20.7 us -> 120 us
  waiting for transfers between devices: 116 us -> 28.7 us
  Pallas kernels: 26.2 us -> 34.9 us
  local copies, waits for them, and re-layouts: 22.6 us -> 30.8 us
  matrix products: 11.7 us -> 15.4 us
    all_gather x0 -> x4, blocking collectives: none -> 98.8 us  [per_device(): grads.append(lax.all_gather(local, 'text', axis=0, tiled=True))]
    reduce_scatter x2 -> x4, waiting for transfers between devices: 67.3 us -> 19.6 us  [per_device(): sums.append(lax.psum_scatter(part, 'text', scatter_dimension=0, tiled=True))]
    all_gather x2 -> x0, waiting for transfers between devices: 39.3 us -> none  [per_device(): grads.append(lax.all_gather(local, 'text', axis=0, tiled=True))]
    pallas_call x2 -> x4, Pallas kernels: 21.6 us -> 30.8 us  [final(): pl.pallas_call(final_kernel, out_shape=jax.ShapeDtypeStruct(logits.shape,...]
    unnamed x25 -> x41, local copies, waits for them, and re-layouts: 13.6 us -> 21.8 us
    dot_general x2 -> x4, matrix products: 11.7 us -> 15.4 us  [per_device(): jnp.dot(spread, weight_q[:, c * width:(c + 1) * width], preferred_element...]
  transfers between devices with their start and end apart: 5 -> 5, of which waited for: 5 -> 5; matrix products, arithmetic and copies ran while one was open for 12% -> 12% of each run, Pallas kernels for 7% -> 1%
where the time goes in v5:
time: 261 us; the launch traced here: 259 us
  blocking collectives  120 us (46%)
  Pallas kernels  34.9 us (13%)
  local copies, waits for them, and re-layouts  30.8 us (12%)
  waiting for transfers between devices  28.7 us (11%)
  matrix products  15.4 us (6%)
  between operations  15.2 us (6%)
  other arithmetic  14.3 us (5%)
    all_gather x4, blocking collectives, per_device(): grads.append(lax.all_gather(local, 'text', axis=0, tiled=True))  98.8 us
    pallas_call x4, Pallas kernels, final(): pl.pallas_call(final_kernel, out_shape=jax.ShapeDtypeStruct(logits.shape,...  30.8 us
    unnamed x41, local copies, waits for them, and re-layouts  21.8 us
    all_to_all x1, blocking collectives, per_device(): lax.all_to_all(own.transpose(1, 0, 2), 'text', split_axis=0, concat_axis=...  20.7 us
    reduce_scatter x4, waiting for transfers between devices, per_device(): sums.append(lax.psum_scatter(part, 'text', scatter_dimension=0, tiled=True))  19.6 us
    dot_general x4, matrix products, per_device(): jnp.dot(spread, weight_q[:, c * width:(c + 1) * width], preferred_element...  15.4 us
    convert_element_type x1, other arithmetic, per_device(): (steps_row * (grid_levels.astype(jnp.float32) + soft)).astype(jnp.bfloat16)  12.8 us
    all_gather x1, waiting for transfers between devices, per_device(): lax.all_gather(own.reshape(n_text * tok_dev, share), 'image', axis=0)  9.03 us
  transfers between devices with their start and end apart: 5, of which 5 were waited for; matrix products, arithmetic and copies ran while one was open for 12% of the time, Pallas kernels for 1%

profile of v5, /device:TPU:0, one launch (start us, length us, event | category | flops | bytes accessed | tf_op | source)
XLA Modules:
  0.0 259.1 jit_solution(8792511111014925873)
XLA Ops:
  6.5 3.2 %copy.20 = bf16[128,8192]{0,1:T(8,128)(2,1)S(1)} copy(bf16[128,8192]{1,0:T(8,128)(2,1)} %param.9) | data formatting | bytes 4194304 | tf_op args[0]
  9.8 0.2 copy.21
  10.1 20.7 %all_to_all.5 = bf16[4,128,512]{2,1,0:T(8,128)(2,1)} all-to-all(bf16[4,128,512]{2,1,0:T(8,128)(2,1)S(1)} %bitcast.36), channel_id=1, replica_groups=mesh['groups'=2,'text'=4,'image'=4] {'text'}, dimensions={0} | all-to-all | bytes 1048576 | tf_op jit(solution)/shard_map/all_to_all | solution.py:178
  30.9 12.8 %multiply_convert_fusion = bf16[2048,2048]{1,0:T(8,128)(2,1)} fusion(f32[2048,2048]{1,0:T(8,128)} %r_ref.7, bf16[2048,2048]{1,0:T(8,128)(2,1)} %param.10, f32[2048]{0:T(1024)S(1)} %copy-done.9), kind=kLoop, calls=%fused_computation | loop fusion | flops 29360128 | bytes 33562624 | tf_op jit(solution)/shard_map/convert_element_type | solution.py:182
  43.6 9.0 %all-gather.2.cloned.1.call-done = bf16[4,512,512]{2,1,0:T(8,128)(2,1)} async-done(((bf16[1,512,512]{2,1,0:T(8,128)(2,1)}), bf16[4,512,512]{2,1,0:T(8,128)(2,1)}) %all-gather.2.cloned.1.call-update) | async-done | bytes 2097168 | tf_op jit(solution)/shard_map/all_gather | solution.py:179
  52.7 2.8 %copy.22 = bf16[512,4,512]{0,2,1:T(8,128)(2,1)S(1)} copy(bf16[512,4,512]{2,0,1:T(8,128)(2,1)} %bitcast.34) | data formatting | bytes 4194304 | tf_op jit(solution)/shard_map/transpose | solution.py:180
  55.4 3.9 %fusion = f32[512,512]{1,0:T(8,128)} fusion(bf16[512,2048]{0,1:T(8,128)(2,1)S(1)} %bitcast.21, bf16[2048,2048]{1,0:T(8,128)(2,1)} %multiply_convert_fusion), kind=kOutput, calls=%fused_computation.1 | convolution fusion | flops 1073741824 | bytes 5242880 | tf_op jit(solution)/shard_map/dot_general | solution.py:205
  59.4 3.8 %fusion.2 = f32[512,512]{1,0:T(8,128)} fusion(bf16[512,2048]{0,1:T(8,128)(2,1)S(1)} %bitcast.22, bf16[2048,2048]{1,0:T(8,128)(2,1)} %multiply_convert_fusion), kind=kOutput, calls=%fused_computation.3 | convolution fusion | flops 1073741824 | bytes 5242880 | tf_op jit(solution)/shard_map/dot_general | solution.py:205
  63.3 3.8 %fusion.4 = f32[512,512]{1,0:T(8,128)} fusion(bf16[512,2048]{0,1:T(8,128)(2,1)S(1)} %bitcast.23, bf16[2048,2048]{1,0:T(8,128)(2,1)} %multiply_convert_fusion), kind=kOutput, calls=%fused_computation.5 | convolution fusion | flops 1073741824 | bytes 5242880 | tf_op jit(solution)/shard_map/dot_general | solution.py:205
  67.6 0.2 select_reduce_fusion.1
  67.8 0.2 select_reduce_fusion
  67.9 3.8 %fusion.6 = f32[512,512]{1,0:T(8,128)} fusion(bf16[512,2048]{0,1:T(8,128)(2,1)S(1)} %bitcast.24, bf16[2048,2048]{1,0:T(8,128)(2,1)} %multiply_convert_fusion), kind=kOutput, calls=%fused_computation.7 | convolution fusion | flops 1073741824 | bytes 5242880 | tf_op jit(solution)/shard_map/dot_general | solution.py:205
  72.0 0.6 slice.16
  72.6 0.6 fusion.9
  74.6 2.7 %constant_dynamic-slice_fusion = (bf16[3202,256]{1,0:T(8,128)(2,1)S(1)}, bf16[3202,256]{1,0:T(8,128)(2,1)S(1)}) fusion(bf16[6404,256]{1,0:T(8,128)(2,1)} %param.14, s32[]{:T(128)S(6)} %select_n.24, bf16[6404,256]{1,0:T(8,128)(2,1)} %param.13), kind=kLoop, calls=%fused_computation.18 | loop fusion | bytes 6557700 | tf_op jit(solution)/shard_map/dynamic_slice | solution.py:195
  77.3 1.3 pad.8.v_ref
  78.6 1.3 pad.7.k_ref
  80.6 6.0 %reduce-scatter.11.cloned.1.call-done.q_ref = f32[128,512]{1,0:T(8,128)} async-done(((f32[512,512]{1,0:T(8,128)}), f32[128,512]{1,0:T(8,128)}) %reduce-scatter.11.cloned.1.call-update) | async-done | bytes 262160 | tf_op jit(solution)/shard_map/reduce_scatter | solution.py:208
  86.6 1.5 copy-done.1
  88.1 1.5 copy-done.5
  89.6 0.9 copy-done.14
  90.5 1.0 attention.7
  91.5 26.4 %all_gather.19.g_ref = bf16[512,512]{1,0:T(8,128)(2,1)S(1)} all-gather(bf16[128,512]{1,0:T(8,128)(2,1)S(1)} %attention.7), channel_id=1, replica_groups=mesh['groups'=2,'text'=4,'image'=4] {'text'}, dimensions={0}, use_global_device_ids=true | all-gather | bytes 655360 | tf_op jit(solution)/shard_map/all_gather | solution.py:211
  117.9 5.4 %reduce-scatter.9.cloned.1.call-done.q_ref = f32[128,512]{1,0:T(8,128)} async-done(((f32[512,512]{1,0:T(8,128)}), f32[128,512]{1,0:T(8,128)}) %reduce-scatter.9.cloned.1.call-update) | async-done | bytes 262160 | tf_op jit(solution)/shard_map/reduce_scatter | solution.py:208
  123.3 1.5 copy-done.2
  124.8 1.5 copy-done.6
  126.2 1.0 copy-done.11
  127.3 0.9 copy-done.15
  128.2 1.0 attention.6
  129.3 26.2 %all_gather.18.g_ref = bf16[512,512]{1,0:T(8,128)(2,1)S(1)} all-gather(bf16[128,512]{1,0:T(8,128)(2,1)S(1)} %attention.6), channel_id=1, replica_groups=mesh['groups'=2,'text'=4,'image'=4] {'text'}, dimensions={0}, use_global_device_ids=true | all-gather | bytes 655360 | tf_op jit(solution)/shard_map/all_gather | solution.py:211
  155.5 4.2 %reduce-scatter.7.cloned.1.call-done.q_ref = f32[128,512]{1,0:T(8,128)} async-done(((f32[512,512]{1,0:T(8,128)}), f32[128,512]{1,0:T(8,128)}) %reduce-scatter.7.cloned.1.call-update) | async-done | bytes 262160 | tf_op jit(solution)/shard_map/reduce_scatter | solution.py:208
  159.7 1.5 copy-done.3
  161.1 1.5 copy-done.7
  162.6 1.0 copy-done.12
  163.6 0.9 copy-done.16
  164.6 1.0 attention.5
  165.6 26.5 %all_gather.17.g_ref = bf16[512,512]{1,0:T(8,128)(2,1)} all-gather(bf16[128,512]{1,0:T(8,128)(2,1)S(1)} %attention.5), channel_id=1, replica_groups=mesh['groups'=2,'text'=4,'image'=4] {'text'}, dimensions={0}, use_global_device_ids=true | all-gather | bytes 655360 | tf_op jit(solution)/shard_map/all_gather | solution.py:211
  192.1 4.1 %reduce-scatter.5.cloned.1.call-done.q_ref = f32[128,512]{1,0:T(8,128)} async-done(((f32[512,512]{1,0:T(8,128)}), f32[128,512]{1,0:T(8,128)}) %reduce-scatter.5.cloned.1.call-update) | async-done | bytes 262160 | tf_op jit(solution)/shard_map/reduce_scatter | solution.py:208
  196.2 1.5 copy-done.4
  197.6 1.5 copy-done.8
  199.1 1.0 copy-done.13
  200.1 0.9 copy-done.17
  201.1 1.0 attention.4
  202.1 19.7 %all_gather.16.g_ref = bf16[512,512]{1,0:T(8,128)(2,1)S(1)} all-gather(bf16[128,512]{1,0:T(8,128)(2,1)S(1)} %attention.4), channel_id=1, replica_groups=mesh['groups'=2,'text'=4,'image'=4] {'text'}, dimensions={0}, use_global_device_ids=true | all-gather | bytes 655360 | tf_op jit(solution)/shard_map/all_gather | solution.py:211
  221.8 7.7 %final.4.rest_0_ = f32[2048,2048]{1,0:T(8,128)} custom-call(bf16[2048,512]{1,0:T(8,128)(2,1)S(1)} %bitcast.25, bf16[512,512]{1,0:T(8,128)(2,1)S(1)} %all_gather.19.g_ref, f32[2048,2048]{1,0:T(8,128)} %r_ref.7, f32[1,2048]{1,0:T(1,128)S(1)} %bitcast.29), custom_call_target="tpu_custom_call" | custom-call | flops 1073741824 | bytes 11010048 | tf_op jit(solution)/shard_map/final/pallas_call | solution.py:135
  229.5 7.7 %final.5.rest_0_ = f32[2048,2048]{1,0:T(8,128)} custom-call(bf16[2048,512]{1,0:T(8,128)(2,1)S(1)} %bitcast.26, bf16[512,512]{1,0:T(8,128)(2,1)S(1)} %all_gather.18.g_ref, f32[2048,2048]{1,0:T(8,128)} %r_ref.7, f32[1,2048]{1,0:T(1,128)S(1)} %bitcast.30, f32[2048,2048]{1,0:T(8,128)} %final.4.rest_0_), custom_call_target="tpu_custom_call", output_to_operand_aliasing={{}: (4, {})} | custom-call | flops 1073741824 | bytes 11010048 | tf_op jit(solution)/shard_map/final/pallas_call | solution.py:135
  237.2 7.7 %final.6.rest_0_ = f32[2048,2048]{1,0:T(8,128)} custom-call(bf16[2048,512]{1,0:T(8,128)(2,1)S(1)} %bitcast.27, bf16[512,512]{1,0:T(8,128)(2,1)S(1)} %copy-done, f32[2048,2048]{1,0:T(8,128)} %r_ref.7, f32[1,2048]{1,0:T(1,128)S(1)} %bitcast.31, f32[2048,2048]{1,0:T(8,128)} %final.5.rest_0_), custom_call_target="tpu_custom_call", output_to_operand_aliasing={{}: (4, {})} | custom-call | flops 1073741824 | bytes 11010048 | tf_op jit(solution)/shard_map/final/pallas_call | solution.py:135
  244.9 7.7 %final.7 = f32[2048,2048]{1,0:T(8,128)} custom-call(bf16[2048,512]{1,0:T(8,128)(2,1)S(1)} %bitcast.28, bf16[512,512]{1,0:T(8,128)(2,1)S(1)} %all_gather.16.g_ref, f32[2048,2048]{1,0:T(8,128)} %r_ref.7, f32[1,2048]{1,0:T(1,128)S(1)} %bitcast.32, f32[2048,2048]{1,0:T(8,128)} %final.6.rest_0_), custom_call_target="tpu_custom_call", output_to_operand_aliasing={{}: (4, {})} | custom-call | flops 1073741824 | bytes 11010048 | tf_op jit(solution)/shard_map/final/pallas_call | solution.py:135
  (41 shorter events, 0.9 us)
Async XLA Ops:
  6.5 46.1 %all-gather.2.cloned.1.call-start = ((), (), s32[]{:S(2)}) async-start(), calls=%async_computation.5 | async-start | bytes 2621440 | tf_op jit(solution)/shard_map/all_gather | solution.py:179
  6.5 24.3 %copy-start.9 = (f32[2048]{0:T(1024)S(1)}, f32[2048]{0:T(1024)}, u32[]{:S(2)}) copy-start(f32[2048]{0:T(1024)} %param.12) | copy-start | bytes 24580
  30.8 55.8 %reduce-scatter.11.cloned.1.call-start = ((), (), s32[]{:S(2)}) async-start(), calls=%async_computation.9 | async-start | bytes 1310720 | tf_op jit(solution)/shard_map/reduce_scatter | solution.py:208
  59.3 64.0 %reduce-scatter.9.cloned.1.call-start = ((), (), s32[]{:S(2)}) async-start(), calls=%async_computation.8 | async-start | bytes 1310720 | tf_op jit(solution)/shard_map/reduce_scatter | solution.py:208
  63.3 4.0 %copy-start.19 = (s32[3]{0:T(128)S(1)}, s32[3]{0:T(128)}, u32[]{:S(2)}) copy-start(s32[3]{0:T(128)} %param.16) | copy-start | bytes 40
  63.3 4.5 %copy-start.18 = (s32[4]{0:T(128)S(1)}, s32[4]{0:T(128)}, u32[]{:S(2)}) copy-start(s32[4]{0:T(128)} %param.17) | copy-start | bytes 52
  63.3 96.4 %reduce-scatter.7.cloned.1.call-start = ((), (), s32[]{:S(2)}) async-start(), calls=%async_computation.7 | async-start | bytes 1310720 | tf_op jit(solution)/shard_map/reduce_scatter | solution.py:208
  67.2 129.0 %reduce-scatter.5.cloned.1.call-start = ((), (), s32[]{:S(2)}) async-start(), calls=%async_computation.6 | async-start | bytes 1310720 | tf_op jit(solution)/shard_map/reduce_scatter | solution.py:208
  77.3 9.4 %copy-start.10 = (bf16[128,2048]{1,0:T(8,128)(2,1)S(1)}, bf16[128,2048]{1,0:T(8,128)(2,1)}, u32[]{:S(2)}) copy-start(bf16[128,2048]{1,0:T(8,128)(2,1)} %t_ref.7) | copy-start | bytes 1572868
  86.6 1.5 copy-start.1
  88.1 1.5 copy-start.5
  89.6 0.9 copy-start.14
  123.3 1.5 copy-start.2
  124.8 1.5 copy-start.6
  126.2 1.0 copy-start.11
  127.3 0.9 copy-start.15
  159.7 1.5 copy-start.3
  161.1 1.5 copy-start.7
  162.6 1.0 copy-start.12
  163.6 0.9 copy-start.16
  196.2 1.5 copy-start.4
  197.6 1.5 copy-start.8
  199.1 1.0 copy-start.13
  200.1 0.9 copy-start.17
  229.5 7.7 %copy-start = (bf16[512,512]{1,0:T(8,128)(2,1)S(1)}, bf16[512,512]{1,0:T(8,128)(2,1)}, u32[]{:S(2)}) copy-start(bf16[512,512]{1,0:T(8,128)(2,1)} %all_gather.17.g_ref) | copy-start | bytes 1572868
Sparse Core Ops, SparseCore 0:
  30.9 21.6 all-gather.1
  59.5 27.1 reduce-scatter.10
  89.0 34.2 reduce-scatter.8
  125.4 34.1 reduce-scatter.6
  161.9 34.2 reduce-scatter.4
